TPU v7x, 128 devices: a whole 4x4x4 slice. The times are simulated.
128 devices in a mesh: depth: 32 (over z, x, core), batch: 4 (over y).
Axes of the slice: x: 4, y: 4, z: 4, core: 2. Of those that a mesh axis runs over, the one named last changes fastest.
Arguments:
- cpoint_guess: float32 [32, 4, 32, 4096], P('depth', 'batch'), may hold values from -6 to 6
- adjoint_guess: float32 [32, 4, 32, 4096], P('depth', 'batch'), may hold values from -6 to 6
- weights: float32 [256, 32, 32], P('depth'), may hold values from -0.5 to 0.5
- biases: float32 [256, 32], P('depth'), may hold values from -3 to 3
- diffusion: float32 [32], replicated, may hold values from 0.02 to 0.25
- section_len: int32 [32], replicated, may hold values from 1 to 8, 96 in all
Outputs:
- states_out: float32 [32, 4, 32, 4096], P('depth', 'batch')
- adjoint_out: float32 [32, 4, 32, 4096], P('depth', 'batch')
- grad_weights: float32 [256, 32, 32], P('depth')
- grad_biases: float32 [256, 32], P('depth')
Inputs may be any that keep to these rules, and one draw needn't show every extreme that they name: `section_len`: each of the 32 sections holds 1 to 8 layers, 96 in all, and one section holds exactly 8.
All inputs are finite; a program needn't handle non-finite values.
Results may differ from a plain program's by a relative error of at most 0.0003.
Values sent between devices are 32-bit elements; how exact they have to be, the bound alone decides.
A program may use at most 128 MiB of HBM per device.

v0:
```python
import jax
import jax.numpy as jnp
from jax import lax
from jax.sharding import PartitionSpec as P

IMG_H = 64
IMG_W = 64
MOST = 8


def from_behind(value, axis, steps):
    count = lax.axis_size(axis)
    initial, last = (max(0, -steps), min(count, count - steps))
    return lax.ppermute(value, axis, [(source, source + steps) for source in range(initial, last)])


def laplace(states):
    shaped = states.reshape(states.shape[:-1] + (IMG_H, IMG_W))
    padded = jnp.pad(shaped, [(0, 0)] * (shaped.ndim - 2) + [(1, 1), (1, 1)])
    beside_all = (
        padded[..., 2:, 1:-1]
        + padded[..., :-2, 1:-1]
        + padded[..., 1:-1, 2:]
        + padded[..., 1:-1, :-2]
    )
    return (beside_all - 4.0 * shaped).reshape(states.shape)


def apply_layer(states, matrix, offset, diffusion, factor):
    pre_act = (
        jnp.einsum("ij,bjp->bip", matrix, states, precision=lax.Precision.HIGHEST)
        + offset[None, :, None]
    )
    mixed = jnp.einsum("ji,bjp->bip", matrix, jnp.tanh(pre_act), precision=lax.Precision.HIGHEST)
    return states + (factor * diffusion)[None, :, None] * laplace(states) - factor * mixed


def fine_factor():
    return jnp.asarray(1.0, jnp.float32) / MOST


def section(states, matrices, offsets, diffusion, layer_count):
    factor = fine_factor()

    def advance(position, current):
        changed = apply_layer(current, matrices[position], offsets[position], diffusion, factor)
        return jnp.where(position < layer_count - 1, changed, current)

    relaxed = lax.fori_loop(0, MOST - 1, advance, states)
    final_slot = layer_count - 1
    return apply_layer(relaxed, matrices[final_slot], offsets[final_slot], diffusion, factor)


def coarse(states, matrix, offset, diffusion, layer_count):
    factor = layer_count.astype(jnp.float32) / MOST
    return apply_layer(states, matrix, offset, diffusion, factor)


def body(cpoint_guess, adjoint_guess, weights, biases, diffusion, section_len):
    own_index = lax.axis_index("depth")
    last_index = lax.axis_size("depth") - 1
    layer_count = section_len[own_index]
    guess_now = cpoint_guess[0]
    pushed = section(guess_now, weights, biases, diffusion, layer_count)
    arrived = from_behind(pushed, "depth", 1)
    cpoints = jnp.where(own_index == 0, guess_now, arrived)
    second = section(cpoints, weights, biases, diffusion, layer_count)
    anchor = coarse(cpoints, weights[0], biases[0], diffusion, layer_count)
    tau_local = second - anchor
    tau_prev = from_behind(tau_local, "depth", 1)

    def relay(position, current):
        propagated = coarse(current, weights[0], biases[0], diffusion, layer_count)
        received = from_behind(propagated, "depth", 1)
        return jnp.where(own_index == 0, cpoints, received + tau_prev)

    states_out = lax.fori_loop(0, lax.axis_size("depth") - 1, relay, cpoints)
    _, pullback = jax.vjp(
        lambda start_state: section(start_state, weights, biases, diffusion, layer_count), cpoints
    )
    lam_start = pullback(adjoint_guess[0])[0]
    from_next = from_behind(lam_start, "depth", -1)
    lam_end = jnp.where(own_index == last_index, adjoint_guess[0], from_next)
    _, pull_full = jax.vjp(
        lambda start_state, mat_all, off_all: section(
            start_state, mat_all, off_all, diffusion, layer_count
        ),
        cpoints,
        weights,
        biases,
    )
    adjoint_here, grad_mats, grad_offs = pull_full(lam_end)
    grad_mats, grad_offs = lax.psum((grad_mats, grad_offs), "batch")
    return (states_out[None], adjoint_here[None], grad_mats, grad_offs)


def solution(mesh):
    placed = (
        P("depth", "batch", None, None),
        P("depth", "batch", None, None),
        P("depth", None, None),
        P("depth", None),
        P(),
        P(),
    )
    return jax.shard_map(
        body,
        mesh=mesh,
        in_specs=placed,
        out_specs=(
            P("depth", "batch", None, None),
            P("depth", "batch", None, None),
            P("depth", None, None),
            P("depth", None),
        ),
        check_vma=False,
    )
```

profile of v0, /device:TPU:64, one launch (start us, length us, event | category | flops | bytes accessed | tf_op | source)
XLA Modules:
  0.0 1197.5 jit_solution(6004343774974952679)
XLA Ops:
  6.3 39.1 %while.132 = (s32[]{:T(128)}, f32[1,32,4096]{2,1,0:T(8,128)S(1)}, s32[]{:T(128)}, f32[32]{0:T(128)}, f32[8,32,32]{2,1,0:T(8,128)}, /*index=5*/f32[8,32]{1,0:T(8,128)}, s32[]{:T(128)}) while((s32[]{:T(128)}, f32[1,32,4096]{2,1,0:T(8,128)S(1)}, s32[]{:T(128)}, f32[32]{0:T(128)}, f32[8,32,32]{2,1,0:T(8,128)}, /*index=5*/f32[8,32]{1,0:T(8,128)}, ...), condition=%wide.region_1.2_spmd, body=%wide.region_0.1_spmd.sunk | while | flops 102105120 | bytes 6325099 | solution.py:49
  55.7 8.6 collective-permute-done.1
  65.8 72.7 %while.133 = (s32[]{:T(128)}, f32[1,32,4096]{2,1,0:T(8,128)S(1)}, s32[]{:T(128)}, f32[32]{0:T(128)S(1)}, f32[8,32,32]{2,1,0:T(8,128)S(1)}, /*index=5*/f32[8,32]{1,0:T(8,128)}, s32[]{:T(128)}) while((s32[]{:T(128)}, f32[1,32,4096]{2,1,0:T(8,128)S(1)}, s32[]{:T(128)}, f32[32]{0:T(128)S(1)}, f32[8,32,32]{2,1,0:T(8,128)S(1)}, ...), condition=%wide.region_3.4_spmd, body=%wide.region_2.3_spmd.sunk | while | flops 102105120 | bytes 6325867 | solution.py:49
  141.7 4.6 fusion.168
  150.2 60.7 %while.135 = (s32[]{:T(128)}, f32[1,32,4096]{2,1,0:T(8,128)S(1)}, f32[7,32,32]{2,1,0:T(8,128)S(1)}, f32[7,1,32,4096]{3,2,1,0:T(8,128)}, pred[7]{0:T(512)(128)(4,...) while((s32[]{:T(128)}, f32[1,32,4096]{2,1,0:T(8,128)S(1)}, ...), condition=%wide.region_7.8_spmd, body=%wide.region_6.7_spmd.sunk | while | flops 102498304 | bytes 6883721 | solution.py:49
  152.4 3.9 fusion.325
  161.1 3.9 fusion.325
  169.8 3.9 fusion.325
  178.4 3.9 fusion.325
  187.1 3.9 fusion.325
  195.8 3.9 fusion.325
  214.9 61.4 %while.136 = (s32[]{:T(128)}, f32[1,32,4096]{2,1,0:T(8,128)S(1)}, pred[7]{0:T(512)(128)(4,1)S(1)}, f32[1,32,1]{1,2,0:T(1,128)S(1)}, f32[7,32,32]{2,1,0:T(8,128)S...) while((s32[]{:T(128)}, f32[1,32,4096]{2,1,0:T(8,128)S(1)}, pred[7]{0:T(512)(128)(4,1)S(1)}, ...), condition=%wide.region_9.10_spmd, body=%wide.region_8.9_spmd.sunk | while | flops 102891520 | bytes 7898350 | solution.py:49
  285.6 74.6 %while.137 = (s32[]{:T(128)}, f32[1,32,4096]{2,1,0:T(8,128)S(1)}, s32[7]{0:T(128)S(1)}, f32[7,32,32]{2,1,0:T(8,128)S(1)}, f32[7,1,32,4096]{3,2,1,0:T(8,128)}, /*...) while((s32[]{:T(128)}, f32[1,32,4096]{2,1,0:T(8,128)S(1)}, ...), condition=%wide.region_11.12_spmd, body=%wide.region_10.11_spmd.sunk | while | flops 102498304 | bytes 8457133 | solution.py:49
  376.1 4.6 fusion.173
  389.2 128.9 %while.138 = (s32[]{:T(128)}, f32[8,32,32]{2,1,0:T(8,128)S(1)}, f32[8,32]{1,0:T(8,128)S(1)}, f32[1,32,4096]{2,1,0:T(8,128)S(1)}, s32[7]{0:T(128)}, /*index=5*/f3...) while((s32[]{:T(128)}, f32[8,32,32]{2,1,0:T(8,128)S(1)}, ...), condition=%wide.region_14.15_spmd, body=%wide.region_12.14_spmd.sunk | while | flops 204081152 | bytes 10050618 | solution.py:49
  522.0 19.2 %all-reduce.24 = (f32[8,32,32]{2,1,0:T(8,128)}, f32[8,32]{1,0:T(8,128)}) all-reduce(f32[8,32,32]{2,1,0:T(8,128)S(1)} %fusion.160, f32[8,32]{1,0:T(8,128)S(1)} %add_any.216), channel_id=1, replica_groups=mesh['depth'=32,'batch'=4] {'batch'}, use_global_device_ids=true, to_apply=%region_15.16 | all-reduce | flops 8448 | bytes 67584 | tf_op jit(solution)/shard_map/psum | solution.py:93
  541.3 655.2 %while.134 = (s32[]{:T(128)}, f32[1,32,4096]{2,1,0:T(8,128)S(1)}, pred[]{:T(512)}, f32[]{:T(128)}, f32[32]{0:T(128)}, /*index=5*/f32[8,32,32]{2,1,0:T(8,128)S(1)...) while((s32[]{:T(128)}, f32[1,32,4096]{2,1,0:T(8,128)S(1)}, pred[]{:T(512)}, ...), condition=%wide.region_5.6_spmd, body=%wide.region_4.5_spmd.sunk | while | flops 102236192 | bytes 10520754 | solution.py:77
  550.6 10.7 collective-permute-done
  571.7 10.7 collective-permute-done
  592.9 10.7 collective-permute-done
  614.0 10.7 collective-permute-done
  635.1 10.7 collective-permute-done
  656.3 10.7 collective-permute-done
  677.4 10.7 collective-permute-done
  698.5 10.7 collective-permute-done
  719.7 10.7 collective-permute-done
  740.8 10.7 collective-permute-done
  762.0 10.7 collective-permute-done
  783.1 10.7 collective-permute-done
  804.2 10.7 collective-permute-done
  825.4 10.7 collective-permute-done
  846.5 10.7 collective-permute-done
  867.6 10.7 collective-permute-done
  888.8 10.7 collective-permute-done
  909.9 10.7 collective-permute-done
  931.1 10.7 collective-permute-done
  952.2 10.7 collective-permute-done
  973.3 10.7 collective-permute-done
  994.5 10.7 collective-permute-done
  1015.6 10.7 collective-permute-done
  1036.7 10.7 collective-permute-done
  1057.9 10.7 collective-permute-done
  1079.0 10.7 collective-permute-done
  1100.2 10.7 collective-permute-done
  1121.3 10.7 collective-permute-done
  1142.4 10.7 collective-permute-done
  1163.6 10.7 collective-permute-done
  1184.7 10.7 collective-permute-done
  (771 shorter events, 798.5 us)
Async XLA Ops:
  45.8 7.6 copy-start.6
  51.5 12.9 %collective-permute-start.1 = (f32[1,32,4096]{2,1,0:T(8,128)}, f32[1,32,4096]{2,1,0:T(8,128)}, u32[]{:S(2)}, u32[]{:S(2)}) collective-permute-start(f32[1,32,4096]{2,1,0:T(8,128)} %fusion.157), channel_id=1, source_target_pairs={{0,4},{4,8},{8,12},{12,16},{16,20},{20,24},{24,28},{28,32},{32,36}... | collective-permute-start | bytes 1572872 | tf_op jit(solution)/shard_map/ppermute | solution.py:14
  54.6 11.2 copy-start.9
  65.6 75.6 %copy-start.2 = (f32[1,32,4096]{2,1,0:T(8,128)}, f32[1,32,4096]{2,1,0:T(8,128)S(1)}, u32[]{:S(2)}) copy-start(f32[1,32,4096]{2,1,0:T(8,128)S(1)} %broadcast_select_fusion) | copy-start | bytes 1572868
  276.4 94.0 %collective-permute-start.3 = (f32[1,32,4096]{2,1,0:T(8,128)S(1)}, f32[1,32,4096]{2,1,0:T(8,128)}, u32[]{:S(2)}, u32[]{:S(2)}) collective-permute-start(f32[1,32,4096]{2,1,0:T(8,128)S(1)} %get-tuple-element.1262), channel_id=1, source_target_pairs={{4,0},{8,4},{12,8},{16,12},{20,16},{24,20},{28,24},{32,28},{36,32}... | collective-permute-start | bytes 1572872 | tf_op jit(solution)/shard_map/ppermute | solution.py:14
  360.2 27.8 %copy-start.11 = (s32[7]{0:T(128)}, s32[7]{0:T(128)S(1)}, u32[]{:S(2)}) copy-start(s32[7]{0:T(128)S(1)} %get-tuple-element.1954) | copy-start | bytes 88
  360.2 8.3 copy-start.3
  370.3 16.1 %copy-start.4 = (f32[4096,32]{0,1:T(8,128)}, f32[4096,32]{0,1:T(8,128)S(1)}, u32[]{:S(2)}) copy-start(f32[4096,32]{0,1:T(8,128)S(1)} %fusion.185) | copy-start | bytes 1572868
  373.5 14.6 %copy-start.7 = (f32[1,32,4096]{2,1,0:T(8,128)}, f32[1,32,4096]{2,1,0:T(8,128)S(1)}, u32[]{:S(2)}) copy-start(f32[1,32,4096]{2,1,0:T(8,128)S(1)} %get-tuple-element.1394) | copy-start | bytes 1572868
  383.0 158.2 %collective-permute-start.2 = (f32[1,32,4096]{2,1,0:T(8,128)}, f32[1,32,4096]{2,1,0:T(8,128)}, u32[]{:S(2)}, u32[]{:S(2)}) collective-permute-start(f32[1,32,4096]{2,1,0:T(8,128)} %get-tuple-element.1404), channel_id=1, source_target_pairs={{0,4},{4,8},{8,12},{12,16},{16,20},{20,24},{24,28},{28,32},{32,36}... | collective-permute-start | bytes 1572872 | tf_op jit(solution)/shard_map/ppermute | solution.py:14
  518.0 23.2 %copy-start = (f32[1,32,4096]{2,1,0:T(8,128)}, f32[1,32,4096]{2,1,0:T(8,128)S(1)}, u32[]{:S(2)}) copy-start(f32[1,32,4096]{2,1,0:T(8,128)S(1)} %get-tuple-element.1270) | copy-start | bytes 1572868
  548.7 12.6 %collective-permute-start = (f32[1,32,4096]{2,1,0:T(8,128)S(1)}, f32[1,32,4096]{2,1,0:T(8,128)S(1)}, u32[]{:S(2)}, u32[]{:S(2)}) collective-permute-start(f32[1,32,4096]{2,1,0:T(8,128)S(1)} %fusion.321), channel_id=1, source_target_pairs={{0,4},{4,8},{8,12},{12,16},{16,20},{20,24},{24,28},{28,32},{32,36}... | collective-permute-start | bytes 1572872 | tf_op jit(solution)/shard_map/while/body/eval_jaxpr/ppermute | solution.py:14
  562.4 6.1 copy-start.10
  569.8 12.6 %collective-permute-start = (f32[1,32,4096]{2,1,0:T(8,128)S(1)}, f32[1,32,4096]{2,1,0:T(8,128)S(1)}, u32[]{:S(2)}, u32[]{:S(2)}) collective-permute-start(f32[1,32,4096]{2,1,0:T(8,128)S(1)} %fusion.321), channel_id=1, source_target_pairs={{0,4},{4,8},{8,12},{12,16},{16,20},{20,24},{24,28},{28,32},{32,36}... | collective-permute-start | bytes 1572872 | tf_op jit(solution)/shard_map/while/body/eval_jaxpr/ppermute | solution.py:14
  590.9 12.6 %collective-permute-start = (f32[1,32,4096]{2,1,0:T(8,128)S(1)}, f32[1,32,4096]{2,1,0:T(8,128)S(1)}, u32[]{:S(2)}, u32[]{:S(2)}) collective-permute-start(f32[1,32,4096]{2,1,0:T(8,128)S(1)} %fusion.321), channel_id=1, source_target_pairs={{0,4},{4,8},{8,12},{12,16},{16,20},{20,24},{24,28},{28,32},{32,36}... | collective-permute-start | bytes 1572872 | tf_op jit(solution)/shard_map/while/body/eval_jaxpr/ppermute | solution.py:14
  612.1 12.6 %collective-permute-start = (f32[1,32,4096]{2,1,0:T(8,128)S(1)}, f32[1,32,4096]{2,1,0:T(8,128)S(1)}, u32[]{:S(2)}, u32[]{:S(2)}) collective-permute-start(f32[1,32,4096]{2,1,0:T(8,128)S(1)} %fusion.321), channel_id=1, source_target_pairs={{0,4},{4,8},{8,12},{12,16},{16,20},{20,24},{24,28},{28,32},{32,36}... | collective-permute-start | bytes 1572872 | tf_op jit(solution)/shard_map/while/body/eval_jaxpr/ppermute | solution.py:14
  633.2 12.6 %collective-permute-start = (f32[1,32,4096]{2,1,0:T(8,128)S(1)}, f32[1,32,4096]{2,1,0:T(8,128)S(1)}, u32[]{:S(2)}, u32[]{:S(2)}) collective-permute-start(f32[1,32,4096]{2,1,0:T(8,128)S(1)} %fusion.321), channel_id=1, source_target_pairs={{0,4},{4,8},{8,12},{12,16},{16,20},{20,24},{24,28},{28,32},{32,36}... | collective-permute-start | bytes 1572872 | tf_op jit(solution)/shard_map/while/body/eval_jaxpr/ppermute | solution.py:14
  654.3 12.6 %collective-permute-start = (f32[1,32,4096]{2,1,0:T(8,128)S(1)}, f32[1,32,4096]{2,1,0:T(8,128)S(1)}, u32[]{:S(2)}, u32[]{:S(2)}) collective-permute-start(f32[1,32,4096]{2,1,0:T(8,128)S(1)} %fusion.321), channel_id=1, source_target_pairs={{0,4},{4,8},{8,12},{12,16},{16,20},{20,24},{24,28},{28,32},{32,36}... | collective-permute-start | bytes 1572872 | tf_op jit(solution)/shard_map/while/body/eval_jaxpr/ppermute | solution.py:14
  675.5 12.6 %collective-permute-start = (f32[1,32,4096]{2,1,0:T(8,128)S(1)}, f32[1,32,4096]{2,1,0:T(8,128)S(1)}, u32[]{:S(2)}, u32[]{:S(2)}) collective-permute-start(f32[1,32,4096]{2,1,0:T(8,128)S(1)} %fusion.321), channel_id=1, source_target_pairs={{0,4},{4,8},{8,12},{12,16},{16,20},{20,24},{24,28},{28,32},{32,36}... | collective-permute-start | bytes 1572872 | tf_op jit(solution)/shard_map/while/body/eval_jaxpr/ppermute | solution.py:14
  689.2 6.1 copy-start.10
  696.6 12.6 %collective-permute-start = (f32[1,32,4096]{2,1,0:T(8,128)S(1)}, f32[1,32,4096]{2,1,0:T(8,128)S(1)}, u32[]{:S(2)}, u32[]{:S(2)}) collective-permute-start(f32[1,32,4096]{2,1,0:T(8,128)S(1)} %fusion.321), channel_id=1, source_target_pairs={{0,4},{4,8},{8,12},{12,16},{16,20},{20,24},{24,28},{28,32},{32,36}... | collective-permute-start | bytes 1572872 | tf_op jit(solution)/shard_map/while/body/eval_jaxpr/ppermute | solution.py:14
  710.4 6.1 copy-start.10
  717.8 12.6 %collective-permute-start = (f32[1,32,4096]{2,1,0:T(8,128)S(1)}, f32[1,32,4096]{2,1,0:T(8,128)S(1)}, u32[]{:S(2)}, u32[]{:S(2)}) collective-permute-start(f32[1,32,4096]{2,1,0:T(8,128)S(1)} %fusion.321), channel_id=1, source_target_pairs={{0,4},{4,8},{8,12},{12,16},{16,20},{20,24},{24,28},{28,32},{32,36}... | collective-permute-start | bytes 1572872 | tf_op jit(solution)/shard_map/while/body/eval_jaxpr/ppermute | solution.py:14
  731.5 6.1 copy-start.10
  738.9 12.6 %collective-permute-start = (f32[1,32,4096]{2,1,0:T(8,128)S(1)}, f32[1,32,4096]{2,1,0:T(8,128)S(1)}, u32[]{:S(2)}, u32[]{:S(2)}) collective-permute-start(f32[1,32,4096]{2,1,0:T(8,128)S(1)} %fusion.321), channel_id=1, source_target_pairs={{0,4},{4,8},{8,12},{12,16},{16,20},{20,24},{24,28},{28,32},{32,36}... | collective-permute-start | bytes 1572872 | tf_op jit(solution)/shard_map/while/body/eval_jaxpr/ppermute | solution.py:14
  752.6 6.1 copy-start.10
  760.0 12.6 %collective-permute-start = (f32[1,32,4096]{2,1,0:T(8,128)S(1)}, f32[1,32,4096]{2,1,0:T(8,128)S(1)}, u32[]{:S(2)}, u32[]{:S(2)}) collective-permute-start(f32[1,32,4096]{2,1,0:T(8,128)S(1)} %fusion.321), channel_id=1, source_target_pairs={{0,4},{4,8},{8,12},{12,16},{16,20},{20,24},{24,28},{28,32},{32,36}... | collective-permute-start | bytes 1572872 | tf_op jit(solution)/shard_map/while/body/eval_jaxpr/ppermute | solution.py:14
  781.2 12.6 %collective-permute-start = (f32[1,32,4096]{2,1,0:T(8,128)S(1)}, f32[1,32,4096]{2,1,0:T(8,128)S(1)}, u32[]{:S(2)}, u32[]{:S(2)}) collective-permute-start(f32[1,32,4096]{2,1,0:T(8,128)S(1)} %fusion.321), channel_id=1, source_target_pairs={{0,4},{4,8},{8,12},{12,16},{16,20},{20,24},{24,28},{28,32},{32,36}... | collective-permute-start | bytes 1572872 | tf_op jit(solution)/shard_map/while/body/eval_jaxpr/ppermute | solution.py:14
  802.3 12.6 %collective-permute-start = (f32[1,32,4096]{2,1,0:T(8,128)S(1)}, f32[1,32,4096]{2,1,0:T(8,128)S(1)}, u32[]{:S(2)}, u32[]{:S(2)}) collective-permute-start(f32[1,32,4096]{2,1,0:T(8,128)S(1)} %fusion.321), channel_id=1, source_target_pairs={{0,4},{4,8},{8,12},{12,16},{16,20},{20,24},{24,28},{28,32},{32,36}... | collective-permute-start | bytes 1572872 | tf_op jit(solution)/shard_map/while/body/eval_jaxpr/ppermute | solution.py:14
  823.4 12.6 %collective-permute-start = (f32[1,32,4096]{2,1,0:T(8,128)S(1)}, f32[1,32,4096]{2,1,0:T(8,128)S(1)}, u32[]{:S(2)}, u32[]{:S(2)}) collective-permute-start(f32[1,32,4096]{2,1,0:T(8,128)S(1)} %fusion.321), channel_id=1, source_target_pairs={{0,4},{4,8},{8,12},{12,16},{16,20},{20,24},{24,28},{28,32},{32,36}... | collective-permute-start | bytes 1572872 | tf_op jit(solution)/shard_map/while/body/eval_jaxpr/ppermute | solution.py:14
  844.6 12.6 %collective-permute-start = (f32[1,32,4096]{2,1,0:T(8,128)S(1)}, f32[1,32,4096]{2,1,0:T(8,128)S(1)}, u32[]{:S(2)}, u32[]{:S(2)}) collective-permute-start(f32[1,32,4096]{2,1,0:T(8,128)S(1)} %fusion.321), channel_id=1, source_target_pairs={{0,4},{4,8},{8,12},{12,16},{16,20},{20,24},{24,28},{28,32},{32,36}... | collective-permute-start | bytes 1572872 | tf_op jit(solution)/shard_map/while/body/eval_jaxpr/ppermute | solution.py:14
  865.7 12.6 %collective-permute-start = (f32[1,32,4096]{2,1,0:T(8,128)S(1)}, f32[1,32,4096]{2,1,0:T(8,128)S(1)}, u32[]{:S(2)}, u32[]{:S(2)}) collective-permute-start(f32[1,32,4096]{2,1,0:T(8,128)S(1)} %fusion.321), channel_id=1, source_target_pairs={{0,4},{4,8},{8,12},{12,16},{16,20},{20,24},{24,28},{28,32},{32,36}... | collective-permute-start | bytes 1572872 | tf_op jit(solution)/shard_map/while/body/eval_jaxpr/ppermute | solution.py:14
  886.9 12.6 %collective-permute-start = (f32[1,32,4096]{2,1,0:T(8,128)S(1)}, f32[1,32,4096]{2,1,0:T(8,128)S(1)}, u32[]{:S(2)}, u32[]{:S(2)}) collective-permute-start(f32[1,32,4096]{2,1,0:T(8,128)S(1)} %fusion.321), channel_id=1, source_target_pairs={{0,4},{4,8},{8,12},{12,16},{16,20},{20,24},{24,28},{28,32},{32,36}... | collective-permute-start | bytes 1572872 | tf_op jit(solution)/shard_map/while/body/eval_jaxpr/ppermute | solution.py:14
  900.6 6.1 copy-start.10
  908.0 12.6 %collective-permute-start = (f32[1,32,4096]{2,1,0:T(8,128)S(1)}, f32[1,32,4096]{2,1,0:T(8,128)S(1)}, u32[]{:S(2)}, u32[]{:S(2)}) collective-permute-start(f32[1,32,4096]{2,1,0:T(8,128)S(1)} %fusion.321), channel_id=1, source_target_pairs={{0,4},{4,8},{8,12},{12,16},{16,20},{20,24},{24,28},{28,32},{32,36}... | collective-permute-start | bytes 1572872 | tf_op jit(solution)/shard_map/while/body/eval_jaxpr/ppermute | solution.py:14
  929.1 12.6 %collective-permute-start = (f32[1,32,4096]{2,1,0:T(8,128)S(1)}, f32[1,32,4096]{2,1,0:T(8,128)S(1)}, u32[]{:S(2)}, u32[]{:S(2)}) collective-permute-start(f32[1,32,4096]{2,1,0:T(8,128)S(1)} %fusion.321), channel_id=1, source_target_pairs={{0,4},{4,8},{8,12},{12,16},{16,20},{20,24},{24,28},{28,32},{32,36}... | collective-permute-start | bytes 1572872 | tf_op jit(solution)/shard_map/while/body/eval_jaxpr/ppermute | solution.py:14
  950.3 12.6 %collective-permute-start = (f32[1,32,4096]{2,1,0:T(8,128)S(1)}, f32[1,32,4096]{2,1,0:T(8,128)S(1)}, u32[]{:S(2)}, u32[]{:S(2)}) collective-permute-start(f32[1,32,4096]{2,1,0:T(8,128)S(1)} %fusion.321), channel_id=1, source_target_pairs={{0,4},{4,8},{8,12},{12,16},{16,20},{20,24},{24,28},{28,32},{32,36}... | collective-permute-start | bytes 1572872 | tf_op jit(solution)/shard_map/while/body/eval_jaxpr/ppermute | solution.py:14
  971.4 12.6 %collective-permute-start = (f32[1,32,4096]{2,1,0:T(8,128)S(1)}, f32[1,32,4096]{2,1,0:T(8,128)S(1)}, u32[]{:S(2)}, u32[]{:S(2)}) collective-permute-start(f32[1,32,4096]{2,1,0:T(8,128)S(1)} %fusion.321), channel_id=1, source_target_pairs={{0,4},{4,8},{8,12},{12,16},{16,20},{20,24},{24,28},{28,32},{32,36}... | collective-permute-start | bytes 1572872 | tf_op jit(solution)/shard_map/while/body/eval_jaxpr/ppermute | solution.py:14
  992.5 12.6 %collective-permute-start = (f32[1,32,4096]{2,1,0:T(8,128)S(1)}, f32[1,32,4096]{2,1,0:T(8,128)S(1)}, u32[]{:S(2)}, u32[]{:S(2)}) collective-permute-start(f32[1,32,4096]{2,1,0:T(8,128)S(1)} %fusion.321), channel_id=1, source_target_pairs={{0,4},{4,8},{8,12},{12,16},{16,20},{20,24},{24,28},{28,32},{32,36}... | collective-permute-start | bytes 1572872 | tf_op jit(solution)/shard_map/while/body/eval_jaxpr/ppermute | solution.py:14
  1013.7 12.6 %collective-permute-start = (f32[1,32,4096]{2,1,0:T(8,128)S(1)}, f32[1,32,4096]{2,1,0:T(8,128)S(1)}, u32[]{:S(2)}, u32[]{:S(2)}) collective-permute-start(f32[1,32,4096]{2,1,0:T(8,128)S(1)} %fusion.321), channel_id=1, source_target_pairs={{0,4},{4,8},{8,12},{12,16},{16,20},{20,24},{24,28},{28,32},{32,36}... | collective-permute-start | bytes 1572872 | tf_op jit(solution)/shard_map/while/body/eval_jaxpr/ppermute | solution.py:14
  1034.8 12.6 %collective-permute-start = (f32[1,32,4096]{2,1,0:T(8,128)S(1)}, f32[1,32,4096]{2,1,0:T(8,128)S(1)}, u32[]{:S(2)}, u32[]{:S(2)}) collective-permute-start(f32[1,32,4096]{2,1,0:T(8,128)S(1)} %fusion.321), channel_id=1, source_target_pairs={{0,4},{4,8},{8,12},{12,16},{16,20},{20,24},{24,28},{28,32},{32,36}... | collective-permute-start | bytes 1572872 | tf_op jit(solution)/shard_map/while/body/eval_jaxpr/ppermute | solution.py:14
  1055.9 12.6 %collective-permute-start = (f32[1,32,4096]{2,1,0:T(8,128)S(1)}, f32[1,32,4096]{2,1,0:T(8,128)S(1)}, u32[]{:S(2)}, u32[]{:S(2)}) collective-permute-start(f32[1,32,4096]{2,1,0:T(8,128)S(1)} %fusion.321), channel_id=1, source_target_pairs={{0,4},{4,8},{8,12},{12,16},{16,20},{20,24},{24,28},{28,32},{32,36}... | collective-permute-start | bytes 1572872 | tf_op jit(solution)/shard_map/while/body/eval_jaxpr/ppermute | solution.py:14
  1077.1 12.6 %collective-permute-start = (f32[1,32,4096]{2,1,0:T(8,128)S(1)}, f32[1,32,4096]{2,1,0:T(8,128)S(1)}, u32[]{:S(2)}, u32[]{:S(2)}) collective-permute-start(f32[1,32,4096]{2,1,0:T(8,128)S(1)} %fusion.321), channel_id=1, source_target_pairs={{0,4},{4,8},{8,12},{12,16},{16,20},{20,24},{24,28},{28,32},{32,36}... | collective-permute-start | bytes 1572872 | tf_op jit(solution)/shard_map/while/body/eval_jaxpr/ppermute | solution.py:14
  1098.2 12.6 %collective-permute-start = (f32[1,32,4096]{2,1,0:T(8,128)S(1)}, f32[1,32,4096]{2,1,0:T(8,128)S(1)}, u32[]{:S(2)}, u32[]{:S(2)}) collective-permute-start(f32[1,32,4096]{2,1,0:T(8,128)S(1)} %fusion.321), channel_id=1, source_target_pairs={{0,4},{4,8},{8,12},{12,16},{16,20},{20,24},{24,28},{28,32},{32,36}... | collective-permute-start | bytes 1572872 | tf_op jit(solution)/shard_map/while/body/eval_jaxpr/ppermute | solution.py:14
  1119.4 12.6 %collective-permute-start = (f32[1,32,4096]{2,1,0:T(8,128)S(1)}, f32[1,32,4096]{2,1,0:T(8,128)S(1)}, u32[]{:S(2)}, u32[]{:S(2)}) collective-permute-start(f32[1,32,4096]{2,1,0:T(8,128)S(1)} %fusion.321), channel_id=1, source_target_pairs={{0,4},{4,8},{8,12},{12,16},{16,20},{20,24},{24,28},{28,32},{32,36}... | collective-permute-start | bytes 1572872 | tf_op jit(solution)/shard_map/while/body/eval_jaxpr/ppermute | solution.py:14
  1140.5 12.6 %collective-permute-start = (f32[1,32,4096]{2,1,0:T(8,128)S(1)}, f32[1,32,4096]{2,1,0:T(8,128)S(1)}, u32[]{:S(2)}, u32[]{:S(2)}) collective-permute-start(f32[1,32,4096]{2,1,0:T(8,128)S(1)} %fusion.321), channel_id=1, source_target_pairs={{0,4},{4,8},{8,12},{12,16},{16,20},{20,24},{24,28},{28,32},{32,36}... | collective-permute-start | bytes 1572872 | tf_op jit(solution)/shard_map/while/body/eval_jaxpr/ppermute | solution.py:14
  1161.6 12.6 %collective-permute-start = (f32[1,32,4096]{2,1,0:T(8,128)S(1)}, f32[1,32,4096]{2,1,0:T(8,128)S(1)}, u32[]{:S(2)}, u32[]{:S(2)}) collective-permute-start(f32[1,32,4096]{2,1,0:T(8,128)S(1)} %fusion.321), channel_id=1, source_target_pairs={{0,4},{4,8},{8,12},{12,16},{16,20},{20,24},{24,28},{28,32},{32,36}... | collective-permute-start | bytes 1572872 | tf_op jit(solution)/shard_map/while/body/eval_jaxpr/ppermute | solution.py:14
  1182.8 12.6 %collective-permute-start = (f32[1,32,4096]{2,1,0:T(8,128)S(1)}, f32[1,32,4096]{2,1,0:T(8,128)S(1)}, u32[]{:S(2)}, u32[]{:S(2)}) collective-permute-start(f32[1,32,4096]{2,1,0:T(8,128)S(1)} %fusion.321), channel_id=1, source_target_pairs={{0,4},{4,8},{8,12},{12,16},{16,20},{20,24},{24,28},{28,32},{32,36}... | collective-permute-start | bytes 1572872 | tf_op jit(solution)/shard_map/while/body/eval_jaxpr/ppermute | solution.py:14
  (28 other events, 159.0 us)
where the time goes:
time: 1210 us; the launch traced here: 1200 us
  waiting for transfers between devices  340 us (28%)
  other arithmetic  297 us (25%)
  local copies, waits for them, and re-layouts  251 us (21%)
  matrix products  217 us (18%)
  starting transfers between devices  66 us (5%)
  blocking collectives  19.2 us (2%)
    ppermute x34, waiting for transfers between devices, from_behind(): lax.ppermute(value, axis, [(source, source + steps) for source in range(i...  340 us
    sub x62, other arithmetic, laplace(): return (beside_all - 4.0 * shaped).reshape(states.shape)  203 us
    dot_general x86, matrix products, apply_layer(): jnp.einsum('ji,bjp->bip', matrix, jnp.tanh(pre_act), precision=lax.Precis...  114 us
    reshape x78, local copies, waits for them, and re-layouts, laplace(): shaped = states.reshape(states.shape[:-1] + (IMG_H, IMG_W))  104 us
    dot_general x88, matrix products, apply_layer(): jnp.einsum('ij,bjp->bip', matrix, states, precision=lax.Precision.HIGHEST)  103 us
    ppermute x34, starting transfers between devices, from_behind(): lax.ppermute(value, axis, [(source, source + steps) for source in range(i...  66 us
    reshape x77, local copies, waits for them, and re-layouts, laplace(): return (beside_all - 4.0 * shaped).reshape(states.shape)  47.6 us
    add x60, local copies, waits for them, and re-layouts, apply_layer(): jnp.einsum('ij,bjp->bip', matrix, states, precision=lax.Precision.HIGHEST)  41.7 us
  transfers between devices with their start and end apart: 34, of which 32 were waited for; matrix products, arithmetic and copies ran while one was open for 19% of the time, Pallas kernels for 0%

commit v1 on v0

v1 whole, which is shorter than its diff:
```python
import jax
import jax.numpy as jnp
from jax import lax
from jax.experimental import pallas as pl
from jax.experimental.pallas import tpu as pltpu
from jax.sharding import PartitionSpec as P

MOST = 8
C = 32
LANES = 128
F = jnp.float32
BF = jnp.bfloat16
NT = (((1,), (1,)), ((), ()))


def split2(x):
    hi = x.astype(BF)
    return hi, (x - hi.astype(F)).astype(BF)


def dot3(packed, x):
    hi, lo = split2(x)
    return jnp.dot(packed, jnp.concatenate([hi, lo, hi], axis=0), preferred_element_type=F)


def pack3(matrix):
    hi, lo = split2(matrix)
    return jnp.concatenate([hi, hi, lo], axis=1)


def lane_masks():
    lane = lax.broadcasted_iota(jnp.int32, (C, LANES), 1)
    return lane < 64, lane % 64 == 0, lane % 64 == 63


def beside(x, masks):
    zero = jnp.zeros_like(x)
    return jnp.where(masks[1], zero, pltpu.roll(x, 1, 1)) + jnp.where(masks[2], zero, pltpu.roll(x, 127, 1))


def chunk_laps(chunks, count, masks):
    turned = [pltpu.roll(x, 64, 1) for x in chunks]
    laps = []
    for k in range(1, count + 1):
        above_below = turned[k] + jnp.where(masks[0], turned[k - 1], turned[k + 1])
        laps.append((above_below + beside(chunks[k], masks)) - 4.0 * chunks[k])
    return laps


def column_of(row, eye):
    return jnp.sum(jnp.where(eye, jnp.broadcast_to(row, (C, C)), 0.0), axis=1, keepdims=True)


def row_of(column, eye):
    return jnp.sum(jnp.where(eye, jnp.broadcast_to(column, (C, C)), 0.0), axis=0, keepdims=True)


def spread(matrix, out_ref):
    for k in range(C):
        out_ref[k] = jnp.broadcast_to(matrix[:, k : k + 1], (C, LANES))


def mix(spread_ref, x, first):
    sums = [first, None]
    for k in range(C):
        term = spread_ref[k] * jnp.broadcast_to(x[k : k + 1, :], (C, LANES))
        sums[k % 2] = term if sums[k % 2] is None else sums[k % 2] + term
    return sums[0] + sums[1]


def kernel(
    guess_ref, adj_ref, w_ref, b_ref, d_ref, n_ref,
    s_out, a_out, gw_out, gb_out,
    A, T, G, LR, PUSH, LSEND, S, S1, S2, TAU_S, TAU_B,
    WC, WT, BB, FD, WP, BP, SPA, SPAT, SPB, SPBT, CB, GB, GR,
    push_s, push_r, lam_s, lam_r, tau_s, tau_r, par_s, par_r, one_s, two_s, st_r, grad_s, grad_r,
):
    sections, images = lax.axis_size("depth"), lax.axis_size("batch")
    d, image = lax.axis_index("depth"), lax.axis_index("batch")
    chunks = guess_ref.shape[1] // LANES
    NB = min(16, chunks)
    blocks = chunks // NB
    core, chip, chips = d % 2, d // 2, sections // 2
    has_prev, has_next = d > 0, d < sections - 1
    even = core == 0
    odd = core == 1
    early, middle = chips // 4, (9 * chips) // 16
    masks = lane_masks()
    eye = lax.broadcasted_iota(jnp.int32, (C, C), 0) == lax.broadcasted_iota(jnp.int32, (C, C), 1)

    def at(c):
        return pl.ds(pl.multiple_of(c * LANES, LANES), LANES)

    def copy(src, dst, ssem, rsem, depth_to, image_to=None):
        return pltpu.make_async_remote_copy(
            src_ref=src, dst_ref=dst, send_sem=ssem, recv_sem=rsem,
            device_id=(depth_to, image if image_to is None else image_to),
            device_id_type=pl.DeviceIdType.MESH,
        )

    barrier = pltpu.get_barrier_semaphore()

    def greet(cond, depth_to, image_to):
        @pl.when(cond)
        def _():
            pl.semaphore_signal(barrier, inc=1, device_id=(depth_to, image_to), device_id_type=pl.DeviceIdType.MESH)

    up2, down2 = jnp.logical_and(even, chip < chips - 1), jnp.logical_and(even, chip > 0)
    greet(has_prev, d - 1, image)
    greet(has_next, d + 1, image)
    greet(up2, d + 2, image)
    greet(down2, d - 2, image)
    for o in range(1, images):
        pl.semaphore_signal(
            barrier, inc=1, device_id=(d, (image + o) % images), device_id_type=pl.DeviceIdType.MESH
        )
    partners = (
        has_prev.astype(jnp.int32) + has_next.astype(jnp.int32) + up2.astype(jnp.int32)
        + down2.astype(jnp.int32) + (images - 1)
    )

    n = n_ref[d]
    diff_col = column_of(d_ref[...], eye)
    diff = jnp.broadcast_to(diff_col, (C, LANES))

    def prepare(i, _):
        factor = jnp.where(i < n, 1.0 / MOST, 0.0)
        WC[i] = pack3(w_ref[i])
        WT[i] = pack3(w_ref[i].T * factor)
        BB[i] = jnp.broadcast_to(column_of(b_ref[pl.ds(i, 1), :], eye), (C, LANES))
        FD[i] = diff * factor
        return 0

    lax.fori_loop(0, MOST, prepare, 0)
    zero_chunk = jnp.zeros((C, LANES), F)
    for l in range(MOST + 1):
        A[l, 0] = zero_chunk
        A[l, chunks + 1] = zero_chunk
    for ref in (G.at[0], G.at[1], LR):
        ref[0] = zero_chunk
        ref[chunks + 1] = zero_chunk
    S[chunks] = zero_chunk
    for c in range(chunks):
        G[0, c + 1] = guess_ref[:, c * LANES : (c + 1) * LANES]

    def forward_block(src, i, j, store, keep):
        u = [src[j * NB + k] for k in range(NB + 2)]
        laps = chunk_laps(u, NB, masks)
        bias = jnp.concatenate([BB[i]] * NB, axis=1)
        act = jnp.tanh(dot3(WC[i], jnp.concatenate(u[1:-1], axis=1)) + bias)
        mixed = dot3(WT[i], act)
        fd = FD[i]
        for k in range(NB):
            store(j * NB + k, u[k + 1] + fd * laps[k] - mixed[:, k * LANES : (k + 1) * LANES])
            if keep is not None:
                keep[j * NB + k] = act[:, k * LANES : (k + 1) * LANES]

    def into(ref, shift):
        def store(c, value):
            ref[c + shift] = value
        return store

    def forward_layer(src, i, store, keep=None, unroll=True):
        def block(j, _):
            forward_block(src, i, j, store, keep)
            return 0
        lax.fori_loop(0, blocks, block, 0, unroll=unroll)

    def first_pass(i, _):
        forward_layer(G.at[i % 2], i, into(G.at[(i + 1) % 2], 1))
        return 0

    lax.fori_loop(0, MOST - 1, first_pass, 0)
    pl.semaphore_wait(barrier, partners)

    def push_copy(j):
        return copy(
            PUSH.at[pl.ds(j * NB, NB)], A.at[0, pl.ds(1 + j * NB, NB)], push_s.at[j], push_r.at[j], d + 1
        )

    def push_block(j, _):
        forward_block(G.at[(MOST - 1) % 2], MOST - 1, j, into(PUSH, 0), None)

        @pl.when(has_next)
        def _():
            push_copy(j).start()
        return 0

    lax.fori_loop(0, blocks, push_block, 0)

    weight_copy = copy(w_ref.at[0], WP, par_s.at[0], par_r.at[0], d - 1)
    bias_copy = copy(b_ref, BP, par_s.at[1], par_r.at[1], d - 1)

    @pl.when(odd)
    def _():
        weight_copy.start()
        bias_copy.start()

    @pl.when(even)
    def _():
        coarse_a = n.astype(F) / MOST
        spread(w_ref[0], SPA)
        spread(w_ref[0].T * coarse_a, SPAT)
        CB[0] = BB[0]
        CB[1] = diff * coarse_a
        weight_copy.wait_recv()
        bias_copy.wait_recv()
        coarse_b = n_ref[d + 1 - core].astype(F) / MOST
        spread(WP[...], SPB)
        spread(WP[...].T * coarse_b, SPBT)
        CB[2] = jnp.broadcast_to(column_of(BP[0:1, :], eye), (C, LANES))
        CB[3] = diff * coarse_b

    @pl.when(has_prev)
    def _():
        for j in range(blocks):
            push_copy(j).wait_recv()

    @pl.when(jnp.logical_not(has_prev))
    def _():
        for c in range(chunks):
            A[0, c + 1] = guess_ref[:, c * LANES : (c + 1) * LANES]

    def second_pass(i, _):
        forward_layer(A.at[i], i, into(A.at[i + 1], 1), T.at[i])
        return 0

    lax.fori_loop(0, MOST, second_pass, 0)

    layers = n.astype(F)

    def tau_of(c):
        start = A[0, c + 1]
        return A[MOST, c + 1] - (start + layers * (A[1, c + 1] - start))

    def tau_copy(j):
        return copy(PUSH2.at[pl.ds(j * NB, NB)], TAU_B.at[pl.ds(j * NB, NB)], tau_s.at[j], tau_r.at[j], d - 1)

    PUSH2 = TAU_S
    sends_tau = jnp.logical_and(odd, has_next)

    @pl.when(sends_tau)
    def _():
        def tau_block(j, _):
            for k in range(NB):
                PUSH2[j * NB + k] = tau_of(j * NB + k)
            tau_copy(j).start()
            return 0
        lax.fori_loop(0, blocks, tau_block, 0)

    @pl.when(even)
    def _():
        before = zero_chunk
        for c in range(chunks):
            turned = pltpu.roll(tau_of(c), 64, 1)
            TAU_S[c] = jnp.where(masks[0], before, turned)
            before = turned
        TAU_S[chunks] = jnp.where(masks[0], before, 0.0)

    def one_copy(c):
        return copy(S1.at[c], S.at[c], one_s.at[c], st_r.at[c], d + 1)

    def two_copy(c):
        return copy(S2.at[c], S.at[c], two_s.at[c], st_r.at[c], d + 2)

    def relay():
        @pl.when(chip == 0)
        def _():
            for c in range(chunks):
                S[c] = guess_ref[:, c * LANES : (c + 1) * LANES]

        @pl.when(chip < chips - 1)
        def _():
            for j in range(blocks):
                tau_copy(j).wait_recv()

        bias_a, fd_a, bias_b, fd_b = CB[0], CB[1], CB[2], CB[3]

        def step(c, carry, first=False, last=False):
            prev, prev_turned, one_prev, one_turned = carry
            if not last:
                @pl.when(chip > 0)
                def _():
                    two_copy(c).wait_recv()
            now = S[c]
            turned = pltpu.roll(now, 64, 1)
            mid = jnp.where(masks[0], prev_turned, turned)
            act = jnp.tanh(mix(SPA, mid, bias_a))
            lap = ((prev + now) + beside(mid, masks)) - 4.0 * mid
            one = (mid + fd_a * lap + TAU_S[c]) - mix(SPAT, act, None)
            if first:
                one = jnp.where(masks[0], 0.0, one)
            if last:
                one = jnp.where(masks[0], one, 0.0)
            turned_one = pltpu.roll(one, 64, 1)
            if not first:
                mid_one = jnp.where(masks[0], one_turned, turned_one)
                S1[c - 1] = mid_one
                one_copy(c - 1).start()

                @pl.when(chip < chips - 1)
                def _():
                    act_b = jnp.tanh(mix(SPB, mid_one, bias_b))
                    lap_b = ((one_prev + one) + beside(mid_one, masks)) - 4.0 * mid_one
                    S2[c - 1] = (mid_one + fd_b * lap_b + TAU_B[c - 1]) - mix(SPBT, act_b, None)
                    two_copy(c - 1).start()
            return now, turned, one, turned_one

        carry = step(0, (zero_chunk,) * 4, first=True)
        carry = lax.fori_loop(1, chunks, step, carry)
        step(chunks, carry, last=True)

    def backward_block(src, i, j, store, with_grads):
        g = [src[j * NB + k] for k in range(NB + 2)]
        laps = chunk_laps(g, NB, masks)
        act = jnp.concatenate([T[i, j * NB + k] for k in range(NB)], axis=1)
        g_hi, g_lo = split2(jnp.concatenate(g[1:-1], axis=1))
        pulled = jnp.dot(WC_T(i), jnp.concatenate([g_hi, g_lo, g_hi], axis=0), preferred_element_type=F)
        pre = (1.0 - act * act) * pulled
        p_hi, p_lo = split2(pre)
        back = jnp.dot(WT[i], jnp.concatenate([p_hi, p_lo, p_hi], axis=0), preferred_element_type=F)
        fd = FD[i]
        for k in range(NB):
            store(j * NB + k, g[k + 1] + fd * laps[k] - back[:, k * LANES : (k + 1) * LANES])
        if not with_grads:
            return None
        t_hi, t_lo = split2(act)
        u_hi, u_lo = split2(jnp.concatenate([A[i, j * NB + k + 1] for k in range(NB)], axis=1))
        left = jnp.concatenate(
            [jnp.concatenate([t_hi, p_hi], axis=1), jnp.concatenate([t_lo, p_lo], axis=1)], axis=0
        )
        right = jnp.concatenate(
            [jnp.concatenate([g_hi, u_hi], axis=1), jnp.concatenate([g_lo, u_lo], axis=1)], axis=0
        )
        prod = lax.dot_general(left, right, NT, preferred_element_type=F)
        bias_sum = pre[:, :LANES]
        for k in range(1, NB):
            bias_sum = bias_sum + pre[:, k * LANES : (k + 1) * LANES]
        return prod, bias_sum

    def WC_T(i):
        return WC[i]

    def lam_copy(j):
        return copy(LSEND.at[pl.ds(j * NB, NB)], LR.at[pl.ds(1 + j * NB, NB)], lam_s.at[j], lam_r.at[j], d - 1)

    def backward_start():
        for c in range(chunks):
            G[0, c + 1] = adj_ref[:, c * LANES : (c + 1) * LANES]

        def layer(i, _):
            def block(j, _):
                backward_block(G.at[i % 2], MOST - 1 - i, j, into(G.at[(i + 1) % 2], 1), False)
                return 0
            lax.fori_loop(0, blocks, block, 0, unroll=True)
            return 0

        lax.fori_loop(0, MOST - 1, layer, 0)

        def block(j, _):
            backward_block(G.at[(MOST - 1) % 2], 0, j, into(LSEND, 0), False)

            @pl.when(has_prev)
            def _():
                lam_copy(j).start()
            return 0

        lax.fori_loop(0, blocks, block, 0)

    def backward_full():
        @pl.when(has_next)
        def _():
            for j in range(blocks):
                lam_copy(j).wait_recv()

        @pl.when(jnp.logical_not(has_next))
        def _():
            for c in range(chunks):
                LR[c + 1] = adj_ref[:, c * LANES : (c + 1) * LANES]

        for c in range(chunks):
            G[0, c + 1] = LR[c + 1]
        GB[MOST] = jnp.zeros((C, C), F)

        def layer(i, _):
            slot = MOST - 1 - i
            factor = jnp.where(slot < n, 1.0 / MOST, 0.0)
            start = (jnp.zeros((2 * C, 2 * C), F), jnp.zeros((C, LANES), F))

            def block(j, sums):
                prod, bias_sum = backward_block(G.at[i % 2], slot, j, into(G.at[(i + 1) % 2], 1), True)
                return sums[0] + prod, sums[1] + bias_sum
            prod, bias_sum = lax.fori_loop(0, blocks, block, start, unroll=True)
            GB[slot] = -factor * (prod[:C, :C] + (prod[:C, C:] + prod[C:, :C]))
            column = jnp.sum(bias_sum, axis=1, keepdims=True)
            GB[MOST, pl.ds(slot, 1), :] = -factor * row_of(column, eye)
            return 0

        lax.fori_loop(0, MOST, layer, 0)
        for c in range(chunks):
            a_out[:, c * LANES : (c + 1) * LANES] = G[0, c + 1]
        GR[image] = GB[...]
        for o in range(1, images):
            grad_copy(o).start()

    def grad_copy(o):
        return copy(GB, GR.at[image], grad_s.at[o - 1], grad_r.at[o - 1], d, (image + o) % images)

    def turn(order, _):
        relay_at = jnp.where(chip < early, 0, jnp.where(chip < middle, 1, 2))
        start_at = jnp.where(jnp.logical_and(even, chip < early), 1, 0)
        full_at = jnp.where(jnp.logical_and(even, chip >= middle), 1, 2)

        @pl.when(jnp.logical_and(even, order == relay_at))
        def _():
            relay()

        @pl.when(order == start_at)
        def _():
            backward_start()

        @pl.when(order == full_at)
        def _():
            backward_full()
        return 0

    lax.fori_loop(0, 3, turn, 0)

    for o in range(1, images):
        grad_copy(o).wait_recv()
    for i in range(MOST + 1):
        total = GR[0, i]
        for b in range(1, images):
            total = total + GR[b, i]
        if i < MOST:
            gw_out[i] = total
        else:
            gb_out[...] = total[:MOST]

    @pl.when(odd)
    def _():
        def take(c, _):
            one_copy(c).wait_recv()
            s_out[:, at(c)] = S[c]
            return 0
        lax.fori_loop(0, chunks, take, 0)

    @pl.when(even)
    def _():
        for c in range(chunks):
            s_out[:, c * LANES : (c + 1) * LANES] = S[c]

    for o in range(1, images):
        grad_copy(o).wait_send()

    @pl.when(has_next)
    def _():
        for j in range(blocks):
            push_copy(j).wait_send()

    @pl.when(has_prev)
    def _():
        for j in range(blocks):
            lam_copy(j).wait_send()

    @pl.when(odd)
    def _():
        weight_copy.wait_send()
        bias_copy.wait_send()

    @pl.when(sends_tau)
    def _():
        for j in range(blocks):
            tau_copy(j).wait_send()

    @pl.when(even)
    def _():
        def sent(c, _):
            one_copy(c).wait_send()
            return 0
        lax.fori_loop(0, chunks, sent, 0)

    @pl.when(up2)
    def _():
        def sent(c, _):
            two_copy(c).wait_send()
            return 0
        lax.fori_loop(0, chunks, sent, 0)


def body(cpoint_guess, adjoint_guess, weights, biases, diffusion, section_len):
    pixels = cpoint_guess.shape[-1]
    images = lax.axis_size("batch")
    chunks = pixels // LANES
    NB = min(16, chunks)
    blocks = chunks // NB
    vmem = pl.BlockSpec(memory_space=pltpu.VMEM)
    image_shape = jax.ShapeDtypeStruct((C, pixels), F)
    dma = pltpu.SemaphoreType.DMA

    def stack(*lead):
        return pltpu.VMEM(lead + (C, LANES), F)

    outs = pl.pallas_call(
        kernel,
        out_shape=(
            image_shape, image_shape,
            jax.ShapeDtypeStruct((MOST, C, C), F), jax.ShapeDtypeStruct((MOST, C), F),
        ),
        in_specs=[vmem] * 5 + [pl.BlockSpec(memory_space=pltpu.SMEM)],
        out_specs=(vmem,) * 4,
        scratch_shapes=[
            stack(MOST + 1, chunks + 2), stack(MOST, chunks), stack(2, chunks + 2), stack(chunks + 2),
            stack(chunks), stack(chunks), stack(chunks + 1), stack(chunks), stack(chunks),
            stack(chunks + 1), stack(chunks),
            pltpu.VMEM((MOST, C, 3 * C), BF), pltpu.VMEM((MOST, C, 3 * C), BF), stack(MOST), stack(MOST),
            pltpu.VMEM((C, C), F), pltpu.VMEM((MOST, C), F),
            stack(C), stack(C), stack(C), stack(C), stack(4),
            pltpu.VMEM((MOST + 1, C, C), F), pltpu.VMEM((images, MOST + 1, C, C), F),
            dma((blocks,)), dma((blocks,)), dma((blocks,)), dma((blocks,)), dma((blocks,)), dma((blocks,)),
            dma((2,)), dma((2,)), dma((chunks,)), dma((chunks,)), dma((chunks,)),
            dma((images - 1,)), dma((images - 1,)),
        ],
        compiler_params=pltpu.CompilerParams(
            collective_id=0, has_side_effects=True, vmem_limit_bytes=56 << 20
        ),
        name="mgrit_cycle",
    )(
        cpoint_guess.reshape(C, pixels), adjoint_guess.reshape(C, pixels), weights, biases,
        diffusion.reshape(1, C), section_len,
    )
    states_out, adjoint_out, grad_weights, grad_biases = outs
    return states_out[None, None], adjoint_out[None, None], grad_weights, grad_biases


def solution(mesh):
    placed = (
        P("depth", "batch", None, None), P("depth", "batch", None, None), P("depth", None, None),
        P("depth", None), P(), P(),
    )
    return jax.shard_map(
        body, mesh=mesh, in_specs=placed,
        out_specs=(
            P("depth", "batch", None, None), P("depth", "batch", None, None), P("depth", None, None),
            P("depth", None),
        ),
        check_vma=False,
    )
```

time: 1210 us -> 87.2 us (0.07)
  the two profiles are of different devices: /device:TPU:64 before, /device:TPU:103 now
where the time goes in v1:
time: 87.2 us; the launch traced here: 86.2 us
  Pallas kernels  81.3 us (93%)
  local copies, waits for them, and re-layouts  4.23 us (5%)
    pallas_call x1, Pallas kernels, body(): pl.pallas_call(kernel, out_shape=(image_shape, image_shape, jax.ShapeDtyp...  81.3 us
    unnamed x10, local copies, waits for them, and re-layouts  4.23 us

profile of v1, /device:TPU:103, one launch (start us, length us, event | category | flops | bytes accessed | tf_op | source)
XLA Modules:
  0.0 86.2 jit_solution(4364802005441830237)
XLA Ops:
  0.6 81.3 %mgrit_cycle.1 = (f32[32,4096]{1,0:T(8,128)}, f32[32,4096]{1,0:T(8,128)}, f32[8,32,32]{2,1,0:T(8,128)}, f32[8,32]{1,0:T(8,128)}) custom-call(f32[32,4096]{1,0:T(8,128)} %bitcast.7, f32[32,4096]{1,0:T(8,128)} %bitcast.8, f32[8,32,32]{2,1,0:T(8,128)} %w_ref.1, f32[8,32]{1,0:T(8,128)} %b_ref.1, f32[1,32]{1,0:T(1,128)} %bitcast.9, s32[32]{0:T(128)} %n_ref.1), custom_call_target="tpu_custom_call" | custom-call | tf_op jit(solution)/shard_map/mgrit_cycle/pallas_call | solution.py:504
  82.0 0.0 copy-start
  82.0 1.9 %copy.14 = f32[1,1,32,4096]{3,2,1,0:T(8,128)} copy(f32[1,1,32,4096]{3,2,1,0:T(8,128)} %bitcast.6) | data formatting | bytes 1048576
  83.9 0.0 copy-done
  83.9 0.0 copy-start.1
  83.9 0.8 copy.15
  84.7 0.2 copy-done.1
  84.9 0.0 copy-start.2
  84.9 0.7 copy.16
  85.6 0.0 copy-done.2
  85.6 0.6 copy.17
Async XLA Ops:
  82.0 1.9 %copy-start = (f32[32,4096]{1,0:T(8,128)S(1)}, f32[32,4096]{1,0:T(8,128)}, u32[]{:S(2)}) copy-start(f32[32,4096]{1,0:T(8,128)} %get-tuple-element.9) | copy-start | bytes 1572868
  83.9 1.0 %copy-start.1 = (f32[8,32,32]{2,1,0:T(8,128)S(1)}, f32[8,32,32]{2,1,0:T(8,128)}, u32[]{:S(2)}) copy-start(f32[8,32,32]{2,1,0:T(8,128)} %get-tuple-element.18) | copy-start | bytes 98308
  84.9 0.7 copy-start.2

commit v2 on v1

--- a/solution.py
+++ b/solution.py
@@ -71,7 +71,7 @@
 def kernel(
     guess_ref, adj_ref, w_ref, b_ref, d_ref, n_ref,
     s_out, a_out, gw_out, gb_out,
-    A, T, G, LR, PUSH, LSEND, S, S1, S2, TAU_S, TAU_B,
+    A, T, G, LR, PUSH, LSEND, S, S2, TAU, TAU_A,
     WC, WT, BB, FD, WP, BP, SPA, SPAT, SPB, SPBT, CB, GB, GR,
     push_s, push_r, lam_s, lam_r, tau_s, tau_r, par_s, par_r, one_s, two_s, st_r, grad_s, grad_r,
 ):
@@ -84,7 +84,7 @@
     has_prev, has_next = d > 0, d < sections - 1
     even = core == 0
     odd = core == 1
-    early, middle = chips // 4, (9 * chips) // 16
+    early, middle = (3 * chips) // 16, (10 * chips) // 16
     masks = lane_masks()
     eye = lax.broadcasted_iota(jnp.int32, (C, C), 0) == lax.broadcasted_iota(jnp.int32, (C, C), 1)
 
@@ -105,7 +105,7 @@
         def _():
             pl.semaphore_signal(barrier, inc=1, device_id=(depth_to, image_to), device_id_type=pl.DeviceIdType.MESH)
 
-    up2, down2 = jnp.logical_and(even, chip < chips - 1), jnp.logical_and(even, chip > 0)
+    up2, down2 = jnp.logical_and(odd, chip < chips - 1), jnp.logical_and(odd, chip > 0)
     greet(has_prev, d - 1, image)
     greet(has_next, d + 1, image)
     greet(up2, d + 2, image)
@@ -139,7 +139,6 @@
     for ref in (G.at[0], G.at[1], LR):
         ref[0] = zero_chunk
         ref[chunks + 1] = zero_chunk
-    S[chunks] = zero_chunk
     for c in range(chunks):
         G[0, c + 1] = guess_ref[:, c * LANES : (c + 1) * LANES]
 
@@ -188,28 +187,40 @@
 
     lax.fori_loop(0, blocks, push_block, 0)
 
-    weight_copy = copy(w_ref.at[0], WP, par_s.at[0], par_r.at[0], d - 1)
-    bias_copy = copy(b_ref, BP, par_s.at[1], par_r.at[1], d - 1)
-
-    @pl.when(odd)
+    weight_copy = copy(w_ref.at[0], WP, par_s.at[0], par_r.at[0], d + 1)
+    bias_copy = copy(b_ref, BP, par_s.at[1], par_r.at[1], d + 1)
+
+    def first_copy(c):
+        return copy(guess_ref.at[:, at(c)], S.at[c], one_s.at[c], st_r.at[c], d + 1)
+
+    starts = jnp.logical_not(has_prev)
+
+    @pl.when(even)
     def _():
         weight_copy.start()
         bias_copy.start()
 
-    @pl.when(even)
-    def _():
-        coarse_a = n.astype(F) / MOST
-        spread(w_ref[0], SPA)
-        spread(w_ref[0].T * coarse_a, SPAT)
-        CB[0] = BB[0]
-        CB[1] = diff * coarse_a
+    @pl.when(starts)
+    def _():
+        def send(c, _):
+            first_copy(c).start()
+            return 0
+        lax.fori_loop(0, chunks, send, 0)
+
+    @pl.when(odd)
+    def _():
+        coarse_b = n.astype(F) / MOST
+        spread(w_ref[0], SPB)
+        spread(w_ref[0].T * -coarse_b, SPBT)
+        CB[2] = BB[0]
+        CB[3] = diff * coarse_b
         weight_copy.wait_recv()
         bias_copy.wait_recv()
-        coarse_b = n_ref[d + 1 - core].astype(F) / MOST
-        spread(WP[...], SPB)
-        spread(WP[...].T * coarse_b, SPBT)
-        CB[2] = jnp.broadcast_to(column_of(BP[0:1, :], eye), (C, LANES))
-        CB[3] = diff * coarse_b
+        coarse_a = n_ref[d - core].astype(F) / MOST
+        spread(WP[...], SPA)
+        spread(WP[...].T * -coarse_a, SPAT)
+        CB[0] = jnp.broadcast_to(column_of(BP[0:1, :], eye), (C, LANES))
+        CB[1] = diff * coarse_a
 
     @pl.when(has_prev)
     def _():
@@ -234,79 +245,65 @@
         return A[MOST, c + 1] - (start + layers * (A[1, c + 1] - start))
 
     def tau_copy(j):
-        return copy(PUSH2.at[pl.ds(j * NB, NB)], TAU_B.at[pl.ds(j * NB, NB)], tau_s.at[j], tau_r.at[j], d - 1)
-
-    PUSH2 = TAU_S
-    sends_tau = jnp.logical_and(odd, has_next)
-
-    @pl.when(sends_tau)
-    def _():
-        def tau_block(j, _):
-            for k in range(NB):
-                PUSH2[j * NB + k] = tau_of(j * NB + k)
-            tau_copy(j).start()
-            return 0
-        lax.fori_loop(0, blocks, tau_block, 0)
+        part = pl.ds(j * NB, NB) if j < blocks else pl.ds(chunks, 1)
+        return copy(TAU.at[part], TAU_A.at[part], tau_s.at[j], tau_r.at[j], d + 1)
 
     @pl.when(even)
     def _():
         before = zero_chunk
         for c in range(chunks):
-            turned = pltpu.roll(tau_of(c), 64, 1)
-            TAU_S[c] = jnp.where(masks[0], before, turned)
-            before = turned
-        TAU_S[chunks] = jnp.where(masks[0], before, 0.0)
+            here = tau_of(c)
+            TAU[c] = jnp.where(masks[0], here, before)
+            before = here
+            if c % NB == NB - 1:
+                tau_copy(c // NB).start()
+        TAU[chunks] = jnp.where(masks[0], 0.0, before)
+        tau_copy(blocks).start()
+
+    @pl.when(odd)
+    def _():
+        for c in range(chunks):
+            TAU[c] = tau_of(c)
 
     def one_copy(c):
-        return copy(S1.at[c], S.at[c], one_s.at[c], st_r.at[c], d + 1)
+        return copy(S.at[c], S.at[c], one_s.at[c], st_r.at[c], d - 1)
 
     def two_copy(c):
         return copy(S2.at[c], S.at[c], two_s.at[c], st_r.at[c], d + 2)
 
-    def relay():
-        @pl.when(chip == 0)
-        def _():
-            for c in range(chunks):
-                S[c] = guess_ref[:, c * LANES : (c + 1) * LANES]
-
-        @pl.when(chip < chips - 1)
-        def _():
-            for j in range(blocks):
-                tau_copy(j).wait_recv()
-
+    def relay(both):
+        for j in range(blocks + 1):
+            tau_copy(j).wait_recv()
         bias_a, fd_a, bias_b, fd_b = CB[0], CB[1], CB[2], CB[3]
+        lower = masks[0]
 
         def step(c, carry, first=False, last=False):
-            prev, prev_turned, one_prev, one_turned = carry
-            if not last:
-                @pl.when(chip > 0)
-                def _():
-                    two_copy(c).wait_recv()
-            now = S[c]
-            turned = pltpu.roll(now, 64, 1)
-            mid = jnp.where(masks[0], prev_turned, turned)
+            prev, one_prev = carry
+            if last:
+                now = zero_chunk
+            else:
+                two_copy(c).wait_recv()
+                one_copy(c).start()
+                now = S[c]
+            mid = jnp.where(lower, now, prev)
+            lap = (pltpu.roll(prev + now, 64, 1) + beside(mid, masks)) - 4.0 * mid
             act = jnp.tanh(mix(SPA, mid, bias_a))
-            lap = ((prev + now) + beside(mid, masks)) - 4.0 * mid
-            one = (mid + fd_a * lap + TAU_S[c]) - mix(SPAT, act, None)
+            one = mix(SPAT, act, mid + fd_a * lap + TAU_A[c])
             if first:
-                one = jnp.where(masks[0], 0.0, one)
+                one = jnp.where(lower, one, 0.0)
             if last:
-                one = jnp.where(masks[0], one, 0.0)
-            turned_one = pltpu.roll(one, 64, 1)
+                one = jnp.where(lower, 0.0, one)
             if not first:
-                mid_one = jnp.where(masks[0], one_turned, turned_one)
-                S1[c - 1] = mid_one
-                one_copy(c - 1).start()
-
-                @pl.when(chip < chips - 1)
-                def _():
+                mid_one = jnp.where(lower, one_prev, one)
+                if both:
+                    lap_b = (pltpu.roll(one_prev + one, 64, 1) + beside(mid_one, masks)) - 4.0 * mid_one
                     act_b = jnp.tanh(mix(SPB, mid_one, bias_b))
-                    lap_b = ((one_prev + one) + beside(mid_one, masks)) - 4.0 * mid_one
-                    S2[c - 1] = (mid_one + fd_b * lap_b + TAU_B[c - 1]) - mix(SPBT, act_b, None)
+                    S2[c - 1] = mix(SPBT, act_b, mid_one + fd_b * lap_b + TAU[c - 1])
                     two_copy(c - 1).start()
-            return now, turned, one, turned_one
-
-        carry = step(0, (zero_chunk,) * 4, first=True)
+                s_out[:, at(c - 1)] = mid_one
+            return now, one
+
+        carry = step(0, (zero_chunk,) * 2, first=True)
         carry = lax.fori_loop(1, chunks, step, carry)
         step(chunks, carry, last=True)
 
@@ -315,7 +312,7 @@
         laps = chunk_laps(g, NB, masks)
         act = jnp.concatenate([T[i, j * NB + k] for k in range(NB)], axis=1)
         g_hi, g_lo = split2(jnp.concatenate(g[1:-1], axis=1))
-        pulled = jnp.dot(WC_T(i), jnp.concatenate([g_hi, g_lo, g_hi], axis=0), preferred_element_type=F)
+        pulled = jnp.dot(WC[i], jnp.concatenate([g_hi, g_lo, g_hi], axis=0), preferred_element_type=F)
         pre = (1.0 - act * act) * pulled
         p_hi, p_lo = split2(pre)
         back = jnp.dot(WT[i], jnp.concatenate([p_hi, p_lo, p_hi], axis=0), preferred_element_type=F)
@@ -338,9 +335,6 @@
             bias_sum = bias_sum + pre[:, k * LANES : (k + 1) * LANES]
         return prod, bias_sum
 
-    def WC_T(i):
-        return WC[i]
-
     def lam_copy(j):
         return copy(LSEND.at[pl.ds(j * NB, NB)], LR.at[pl.ds(1 + j * NB, NB)], lam_s.at[j], lam_r.at[j], d - 1)
 
@@ -408,12 +402,17 @@
 
     def turn(order, _):
         relay_at = jnp.where(chip < early, 0, jnp.where(chip < middle, 1, 2))
-        start_at = jnp.where(jnp.logical_and(even, chip < early), 1, 0)
-        full_at = jnp.where(jnp.logical_and(even, chip >= middle), 1, 2)
-
-        @pl.when(jnp.logical_and(even, order == relay_at))
-        def _():
-            relay()
+        start_at = jnp.where(jnp.logical_and(odd, chip < early), 1, 0)
+        full_at = jnp.where(jnp.logical_and(odd, chip >= middle), 1, 2)
+        here = jnp.logical_and(odd, order == relay_at)
+
+        @pl.when(jnp.logical_and(here, chip < chips - 1))
+        def _():
+            relay(True)
+
+        @pl.when(jnp.logical_and(here, chip == chips - 1))
+        def _():
+            relay(False)
 
         @pl.when(order == start_at)
         def _():
@@ -437,7 +436,7 @@
         else:
             gb_out[...] = total[:MOST]
 
-    @pl.when(odd)
+    @pl.when(even)
     def _():
         def take(c, _):
             one_copy(c).wait_recv()
@@ -445,11 +444,6 @@
             return 0
         lax.fori_loop(0, chunks, take, 0)
 
-    @pl.when(even)
-    def _():
-        for c in range(chunks):
-            s_out[:, c * LANES : (c + 1) * LANES] = S[c]
-
     for o in range(1, images):
         grad_copy(o).wait_send()
 
@@ -463,17 +457,21 @@
         for j in range(blocks):
             lam_copy(j).wait_send()
 
-    @pl.when(odd)
+    @pl.when(even)
     def _():
         weight_copy.wait_send()
         bias_copy.wait_send()
-
-    @pl.when(sends_tau)
-    def _():
-        for j in range(blocks):
+        for j in range(blocks + 1):
             tau_copy(j).wait_send()
 
-    @pl.when(even)
+    @pl.when(starts)
+    def _():
+        def sent(c, _):
+            first_copy(c).wait_send()
+            return 0
+        lax.fori_loop(0, chunks, sent, 0)
+
+    @pl.when(odd)
     def _():
         def sent(c, _):
             one_copy(c).wait_send()
@@ -511,13 +509,12 @@
         out_specs=(vmem,) * 4,
         scratch_shapes=[
             stack(MOST + 1, chunks + 2), stack(MOST, chunks), stack(2, chunks + 2), stack(chunks + 2),
-            stack(chunks), stack(chunks), stack(chunks + 1), stack(chunks), stack(chunks),
-            stack(chunks + 1), stack(chunks),
+            stack(chunks), stack(chunks), stack(chunks), stack(chunks), stack(chunks + 1), stack(chunks + 1),
             pltpu.VMEM((MOST, C, 3 * C), BF), pltpu.VMEM((MOST, C, 3 * C), BF), stack(MOST), stack(MOST),
             pltpu.VMEM((C, C), F), pltpu.VMEM((MOST, C), F),
             stack(C), stack(C), stack(C), stack(C), stack(4),
             pltpu.VMEM((MOST + 1, C, C), F), pltpu.VMEM((images, MOST + 1, C, C), F),
-            dma((blocks,)), dma((blocks,)), dma((blocks,)), dma((blocks,)), dma((blocks,)), dma((blocks,)),
+            dma((blocks,)), dma((blocks,)), dma((blocks,)), dma((blocks,)), dma((blocks + 1,)), dma((blocks + 1,)),
             dma((2,)), dma((2,)), dma((chunks,)), dma((chunks,)), dma((chunks,)),
             dma((images - 1,)), dma((images - 1,)),
         ],

time: 87.2 us -> 72 us (0.83)
  the two profiles are of different devices: /device:TPU:103 before, /device:TPU:67 now
where the time goes in v2:
time: 72 us; the launch traced here: 71.8 us
  Pallas kernels  67 us (93%)
  local copies, waits for them, and re-layouts  4.23 us (6%)
    pallas_call x1, Pallas kernels, body(): pl.pallas_call(kernel, out_shape=(image_shape, image_shape, jax.ShapeDtyp...  67 us
    unnamed x10, local copies, waits for them, and re-layouts  4.23 us

profile of v2, /device:TPU:67, one launch (start us, length us, event | category | flops | bytes accessed | tf_op | source)
XLA Modules:
  0.0 71.8 jit_solution(12505708789566718275)
XLA Ops:
  0.6 67.0 %mgrit_cycle.1 = (f32[32,4096]{1,0:T(8,128)}, f32[32,4096]{1,0:T(8,128)}, f32[8,32,32]{2,1,0:T(8,128)}, f32[8,32]{1,0:T(8,128)}) custom-call(f32[32,4096]{1,0:T(8,128)} %bitcast.7, f32[32,4096]{1,0:T(8,128)} %bitcast.8, f32[8,32,32]{2,1,0:T(8,128)} %w_ref.1, f32[8,32]{1,0:T(8,128)} %b_ref.1, f32[1,32]{1,0:T(1,128)} %bitcast.9, s32[32]{0:T(128)} %n_ref.1), custom_call_target="tpu_custom_call" | custom-call | tf_op jit(solution)/shard_map/mgrit_cycle/pallas_call | solution.py:502
  67.6 0.0 copy-start
  67.6 1.9 %copy.14 = f32[1,1,32,4096]{3,2,1,0:T(8,128)} copy(f32[1,1,32,4096]{3,2,1,0:T(8,128)} %bitcast.6) | data formatting | bytes 1048576
  69.5 0.0 copy-done
  69.5 0.0 copy-start.1
  69.5 0.8 %copy.15 = f32[1,1,32,4096]{3,2,1,0:T(8,128)} copy(f32[1,1,32,4096]{3,2,1,0:T(8,128)S(1)} %bitcast.5) | data formatting | bytes 1048576
  70.3 0.2 copy-done.1
  70.6 0.0 copy-start.2
  70.6 0.7 copy.16
  71.2 0.0 copy-done.2
  71.2 0.6 copy.17
Async XLA Ops:
  67.6 1.9 %copy-start = (f32[32,4096]{1,0:T(8,128)S(1)}, f32[32,4096]{1,0:T(8,128)}, u32[]{:S(2)}) copy-start(f32[32,4096]{1,0:T(8,128)} %get-tuple-element.9) | copy-start | bytes 1572868
  69.5 1.0 %copy-start.1 = (f32[8,32,32]{2,1,0:T(8,128)S(1)}, f32[8,32,32]{2,1,0:T(8,128)}, u32[]{:S(2)}) copy-start(f32[8,32,32]{2,1,0:T(8,128)} %get-tuple-element.18) | copy-start | bytes 98308
  70.6 0.7 copy-start.2

commit v3 on v2

--- a/solution.py
+++ b/solution.py
@@ -84,7 +84,7 @@
     has_prev, has_next = d > 0, d < sections - 1
     even = core == 0
     odd = core == 1
-    early, middle = (3 * chips) // 16, (10 * chips) // 16
+    early, middle = (3 * chips) // 16, chips // 2
     masks = lane_masks()
     eye = lax.broadcasted_iota(jnp.int32, (C, C), 0) == lax.broadcasted_iota(jnp.int32, (C, C), 1)
 
@@ -486,6 +486,15 @@
         lax.fori_loop(0, chunks, sent, 0)
 
 
+def write_out(*refs):
+    sems = refs[8]
+    copies = [pltpu.make_async_copy(refs[i], refs[i + 4], sems.at[i]) for i in range(4)]
+    for one in copies:
+        one.start()
+    for one in copies:
+        one.wait()
+
+
 def body(cpoint_guess, adjoint_guess, weights, biases, diffusion, section_len):
     pixels = cpoint_guess.shape[-1]
     images = lax.axis_size("batch")
@@ -519,14 +528,22 @@
             dma((images - 1,)), dma((images - 1,)),
         ],
         compiler_params=pltpu.CompilerParams(
-            collective_id=0, has_side_effects=True, vmem_limit_bytes=56 << 20
+            collective_id=0, has_side_effects=True, vmem_limit_bytes=24 << 20
         ),
         name="mgrit_cycle",
     )(
         cpoint_guess.reshape(C, pixels), adjoint_guess.reshape(C, pixels), weights, biases,
         diffusion.reshape(1, C), section_len,
     )
-    states_out, adjoint_out, grad_weights, grad_biases = outs
+    states_out, adjoint_out, grad_weights, grad_biases = pl.pallas_call(
+        write_out,
+        out_shape=tuple(jax.ShapeDtypeStruct(o.shape, o.dtype) for o in outs),
+        in_specs=[vmem] * 4,
+        out_specs=(pl.BlockSpec(memory_space=pltpu.HBM),) * 4,
+        scratch_shapes=[dma((4,))],
+        compiler_params=pltpu.CompilerParams(vmem_limit_bytes=8 << 20),
+        name="write_out",
+    )(*outs)
     return states_out[None, None], adjoint_out[None, None], grad_weights, grad_biases
 
 

time: 72 us -> 70.9 us (0.985)
  the two profiles are of different devices: /device:TPU:67 before, /device:TPU:103 now
where the time goes in v3:
time: 70.9 us; the launch traced here: 70.7 us
  Pallas kernels  66.3 us (94%)
  local copies, waits for them, and re-layouts  3.66 us (5%)
    pallas_call x1, Pallas kernels, body(): pl.pallas_call(kernel, out_shape=(image_shape, image_shape, jax.ShapeDtyp...  65.3 us
    unnamed x12, local copies, waits for them, and re-layouts  3.66 us

profile of v3, /device:TPU:103, one launch (start us, length us, event | category | flops | bytes accessed | tf_op | source)
XLA Modules:
  0.0 70.7 jit_solution(17819647210125877497)
XLA Ops:
  0.6 0.0 copy-start.3
  0.6 0.0 copy-start.4
  0.7 0.0 copy-start.5
  0.7 0.7 copy-done.3
  1.3 0.0 copy-done.4
  1.3 0.0 copy-done.5
  1.3 0.0 copy-start
  1.3 1.0 %copy-done = f32[1,1,32,4096]{3,2,1,0:T(8,128)S(1)} copy-done((f32[1,1,32,4096]{3,2,1,0:T(8,128)S(1)}, f32[1,1,32,4096]{3,2,1,0:T(8,128)}, u32[]{:S(2)}) %copy-start) | copy-done | bytes 524312
  2.4 0.0 copy-start.1
  2.4 1.0 %copy-done.1 = f32[1,1,32,4096]{3,2,1,0:T(8,128)S(1)} copy-done((f32[1,1,32,4096]{3,2,1,0:T(8,128)S(1)}, f32[1,1,32,4096]{3,2,1,0:T(8,128)}, u32[]{:S(2)}) %copy-start.1) | copy-done | bytes 524312
  3.4 0.0 copy-start.2
  3.4 0.9 %copy-done.2 = f32[8,32,32]{2,1,0:T(8,128)S(1)} copy-done((f32[8,32,32]{2,1,0:T(8,128)S(1)}, f32[8,32,32]{2,1,0:T(8,128)}, u32[]{:S(2)}) %copy-start.2) | copy-done | bytes 32792
  4.3 65.3 %mgrit_cycle.1 = (f32[32,4096]{1,0:T(8,128)S(1)}, f32[32,4096]{1,0:T(8,128)S(1)}, f32[8,32,32]{2,1,0:T(8,128)S(1)}, f32[8,32]{1,0:T(8,128)S(1)}) custom-call(f32[32,4096]{1,0:T(8,128)S(1)} %bitcast.5, f32[32,4096]{1,0:T(8,128)S(1)} %bitcast.6, f32[8,32,32]{2,1,0:T(8,128)S(1)} %copy-done.2, f32[8,32]{1,0:T(8,128)S(1)} %copy-done.3, f32[1,32]{1,0:T(1,128)S(1)} %bitcast.7, ...), custom_call_target="tpu_custom_call" | custom-call | tf_op jit(solution)/shard_map/mgrit_cycle/pallas_call | solution.py:511
  69.6 1.0 %write_out.1 = (f32[32,4096]{1,0:T(8,128)}, f32[32,4096]{1,0:T(8,128)}, f32[8,32,32]{2,1,0:T(8,128)}, f32[8,32]{1,0:T(8,128)}) custom-call(f32[32,4096]{1,0:T(8,128)S(1)} %get-tuple-element.12.refs_0_, f32[32,4096]{1,0:T(8,128)S(1)} %get-tuple-element.13.refs_1_, f32[8,32,32]{2,1,0:T(8,128)S(1)} %get-tuple-element.14.refs_2_, ...), custom_call_target="tpu_custom_call" | custom-call | tf_op jit(solution)/shard_map/write_out/pallas_call | solution.py:538
Async XLA Ops:
  0.6 0.7 copy-start.3
  0.6 0.7 copy-start.4
  0.7 0.7 copy-start.5
  1.3 1.0 %copy-start = (f32[1,1,32,4096]{3,2,1,0:T(8,128)S(1)}, f32[1,1,32,4096]{3,2,1,0:T(8,128)}, u32[]{:S(2)}) copy-start(f32[1,1,32,4096]{3,2,1,0:T(8,128)} %param.6) | copy-start | bytes 1572868
  2.4 1.0 %copy-start.1 = (f32[1,1,32,4096]{3,2,1,0:T(8,128)S(1)}, f32[1,1,32,4096]{3,2,1,0:T(8,128)}, u32[]{:S(2)}) copy-start(f32[1,1,32,4096]{3,2,1,0:T(8,128)} %param.7) | copy-start | bytes 1572868
  3.4 0.9 %copy-start.2 = (f32[8,32,32]{2,1,0:T(8,128)S(1)}, f32[8,32,32]{2,1,0:T(8,128)}, u32[]{:S(2)}) copy-start(f32[8,32,32]{2,1,0:T(8,128)} %w_ref.1) | copy-start | bytes 98308

commit v4 on v3

--- a/solution.py
+++ b/solution.py
@@ -69,11 +69,12 @@
 
 
 def kernel(
-    guess_ref, adj_ref, w_ref, b_ref, d_ref, n_ref,
+    guess_ref, adj_ref, w_hbm, b_hbm, d_hbm, n_hbm,
     s_out, a_out, gw_out, gb_out,
     A, T, G, LR, PUSH, LSEND, S, S2, TAU, TAU_A,
     WC, WT, BB, FD, WP, BP, SPA, SPAT, SPB, SPBT, CB, GB, GR,
     push_s, push_r, lam_s, lam_r, tau_s, tau_r, par_s, par_r, one_s, two_s, st_r, grad_s, grad_r,
+    w_ref, b_ref, d_ref, n_ref, in_s, guess_s, adj_s, spare_s,
 ):
     sections, images = lax.axis_size("depth"), lax.axis_size("batch")
     d, image = lax.axis_index("depth"), lax.axis_index("batch")
@@ -98,6 +99,36 @@
             device_id_type=pl.DeviceIdType.MESH,
         )
 
+    def brought(src, dst, sem):
+        return pltpu.make_async_copy(src, dst, sem)
+
+    def guess_in(c):
+        return brought(guess_ref.at[:, at(c)], G.at[0, c + 1], guess_s.at[c])
+
+    def guess_start(c):
+        return brought(guess_ref.at[:, at(c)], A.at[0, c + 1], spare_s.at[c])
+
+    def adj_in(c):
+        return brought(adj_ref.at[:, at(c)], G.at[0, c + 1], adj_s.at[c])
+
+    def adj_end(c):
+        return brought(adj_ref.at[:, at(c)], LR.at[c + 1], spare_s.at[c])
+
+    def each_chunk(action):
+        def one(c, _):
+            action(c)
+            return 0
+        lax.fori_loop(0, chunks, one, 0)
+
+    small = [
+        brought(src, dst, in_s.at[i])
+        for i, (src, dst) in enumerate(((n_hbm, n_ref), (w_hbm, w_ref), (b_hbm, b_ref), (d_hbm, d_ref)))
+    ]
+    for part in small:
+        part.start()
+    for c in range(chunks):
+        guess_in(c).start()
+
     barrier = pltpu.get_barrier_semaphore()
 
     def greet(cond, depth_to, image_to):
@@ -119,6 +150,26 @@
         + down2.astype(jnp.int32) + (images - 1)
     )
 
+    starts, ends = jnp.logical_not(has_prev), jnp.logical_not(has_next)
+
+    @pl.when(starts)
+    def _():
+        each_chunk(lambda c: guess_start(c).start())
+
+    @pl.when(ends)
+    def _():
+        each_chunk(lambda c: adj_end(c).start())
+
+    zero_chunk = jnp.zeros((C, LANES), F)
+    for l in range(MOST + 1):
+        A[l, 0] = zero_chunk
+        A[l, chunks + 1] = zero_chunk
+    for ref in (G.at[0], G.at[1], LR):
+        ref[0] = zero_chunk
+        ref[chunks + 1] = zero_chunk
+
+    for part in small:
+        part.wait()
     n = n_ref[d]
     diff_col = column_of(d_ref[...], eye)
     diff = jnp.broadcast_to(diff_col, (C, LANES))
@@ -131,16 +182,9 @@
         FD[i] = diff * factor
         return 0
 
-    lax.fori_loop(0, MOST, prepare, 0)
-    zero_chunk = jnp.zeros((C, LANES), F)
-    for l in range(MOST + 1):
-        A[l, 0] = zero_chunk
-        A[l, chunks + 1] = zero_chunk
-    for ref in (G.at[0], G.at[1], LR):
-        ref[0] = zero_chunk
-        ref[chunks + 1] = zero_chunk
+    lax.fori_loop(0, MOST, prepare, 0, unroll=True)
     for c in range(chunks):
-        G[0, c + 1] = guess_ref[:, c * LANES : (c + 1) * LANES]
+        guess_in(c).wait()
 
     def forward_block(src, i, j, store, keep):
         u = [src[j * NB + k] for k in range(NB + 2)]
@@ -186,14 +230,14 @@
         return 0
 
     lax.fori_loop(0, blocks, push_block, 0)
+    for c in range(chunks):
+        adj_in(c).start()
 
     weight_copy = copy(w_ref.at[0], WP, par_s.at[0], par_r.at[0], d + 1)
     bias_copy = copy(b_ref, BP, par_s.at[1], par_r.at[1], d + 1)
 
     def first_copy(c):
         return copy(guess_ref.at[:, at(c)], S.at[c], one_s.at[c], st_r.at[c], d + 1)
-
-    starts = jnp.logical_not(has_prev)
 
     @pl.when(even)
     def _():
@@ -227,10 +271,9 @@
         for j in range(blocks):
             push_copy(j).wait_recv()
 
-    @pl.when(jnp.logical_not(has_prev))
-    def _():
-        for c in range(chunks):
-            A[0, c + 1] = guess_ref[:, c * LANES : (c + 1) * LANES]
+    @pl.when(starts)
+    def _():
+        each_chunk(lambda c: guess_start(c).wait())
 
     def second_pass(i, _):
         forward_layer(A.at[i], i, into(A.at[i + 1], 1), T.at[i])
@@ -272,8 +315,6 @@
         return copy(S2.at[c], S.at[c], two_s.at[c], st_r.at[c], d + 2)
 
     def relay(both):
-        for j in range(blocks + 1):
-            tau_copy(j).wait_recv()
         bias_a, fd_a, bias_b, fd_b = CB[0], CB[1], CB[2], CB[3]
         lower = masks[0]
 
@@ -303,8 +344,13 @@
                 s_out[:, at(c - 1)] = mid_one
             return now, one
 
+        tau_copy(0).wait_recv()
         carry = step(0, (zero_chunk,) * 2, first=True)
-        carry = lax.fori_loop(1, chunks, step, carry)
+        for j in range(blocks):
+            if j:
+                tau_copy(j).wait_recv()
+            carry = lax.fori_loop(max(1, j * NB), (j + 1) * NB, step, carry)
+        tau_copy(blocks).wait_recv()
         step(chunks, carry, last=True)
 
     def backward_block(src, i, j, store, with_grads):
@@ -340,7 +386,7 @@
 
     def backward_start():
         for c in range(chunks):
-            G[0, c + 1] = adj_ref[:, c * LANES : (c + 1) * LANES]
+            adj_in(c).wait()
 
         def layer(i, _):
             def block(j, _):
@@ -367,10 +413,9 @@
             for j in range(blocks):
                 lam_copy(j).wait_recv()
 
-        @pl.when(jnp.logical_not(has_next))
-        def _():
-            for c in range(chunks):
-                LR[c + 1] = adj_ref[:, c * LANES : (c + 1) * LANES]
+        @pl.when(ends)
+        def _():
+            each_chunk(lambda c: adj_end(c).wait())
 
         for c in range(chunks):
             G[0, c + 1] = LR[c + 1]
@@ -514,7 +559,7 @@
             image_shape, image_shape,
             jax.ShapeDtypeStruct((MOST, C, C), F), jax.ShapeDtypeStruct((MOST, C), F),
         ),
-        in_specs=[vmem] * 5 + [pl.BlockSpec(memory_space=pltpu.SMEM)],
+        in_specs=[pl.BlockSpec(memory_space=pltpu.HBM)] * 6,
         out_specs=(vmem,) * 4,
         scratch_shapes=[
             stack(MOST + 1, chunks + 2), stack(MOST, chunks), stack(2, chunks + 2), stack(chunks + 2),
@@ -526,14 +571,21 @@
             dma((blocks,)), dma((blocks,)), dma((blocks,)), dma((blocks,)), dma((blocks + 1,)), dma((blocks + 1,)),
             dma((2,)), dma((2,)), dma((chunks,)), dma((chunks,)), dma((chunks,)),
             dma((images - 1,)), dma((images - 1,)),
+            pltpu.VMEM((MOST, C, C), F), pltpu.VMEM((MOST, C), F), pltpu.VMEM((1, C), F),
+            pltpu.SMEM(section_len.shape, jnp.int32), dma((4,)), dma((chunks,)), dma((chunks,)), dma((chunks,)),
         ],
         compiler_params=pltpu.CompilerParams(
             collective_id=0, has_side_effects=True, vmem_limit_bytes=24 << 20
         ),
         name="mgrit_cycle",
     )(
-        cpoint_guess.reshape(C, pixels), adjoint_guess.reshape(C, pixels), weights, biases,
-        diffusion.reshape(1, C), section_len,
+        *(
+            pltpu.with_memory_space_constraint(x, pltpu.HBM)
+            for x in (
+                cpoint_guess.reshape(C, pixels), adjoint_guess.reshape(C, pixels), weights, biases,
+                diffusion.reshape(1, C), section_len,
+            )
+        )
     )
     states_out, adjoint_out, grad_weights, grad_biases = pl.pallas_call(
         write_out,

time: 70.9 us -> 67.9 us (0.958)
  local copies, waits for them, and re-layouts: 3.66 us -> 0 us
  Pallas kernels: 66.3 us -> 67.1 us
    unnamed x12 -> x0, local copies, waits for them, and re-layouts: 3.66 us -> none
    pallas_call x1, Pallas kernels: 65.3 us -> 66.1 us  [body(): pl.pallas_call(kernel, out_shape=(image_shape, image_shape, jax.ShapeDtyp...]
where the time goes in v4:
time: 67.9 us; the launch traced here: 67.7 us
  Pallas kernels  67.1 us (99%)
    pallas_call x1, Pallas kernels, body(): pl.pallas_call(kernel, out_shape=(image_shape, image_shape, jax.ShapeDtyp...  66.1 us

profile of v4, /device:TPU:103, one launch (start us, length us, event | category | flops | bytes accessed | tf_op | source)
XLA Modules:
  0.0 67.7 jit_solution(16583557555520347437)
XLA Ops:
  0.6 66.1 %mgrit_cycle.1 = (f32[32,4096]{1,0:T(8,128)S(1)}, f32[32,4096]{1,0:T(8,128)S(1)}, f32[8,32,32]{2,1,0:T(8,128)S(1)}, f32[8,32]{1,0:T(8,128)S(1)}) custom-call(f32[32,4096]{1,0:T(8,128)} %bitcast.5, f32[32,4096]{1,0:T(8,128)} %bitcast.6, f32[8,32,32]{2,1,0:T(8,128)} %w_hbm.1, f32[8,32]{1,0:T(8,128)} %b_hbm.1, f32[1,32]{1,0:T(1,128)} %bitcast.7, s32[32]{0:T(128)} %n_hbm.1), custom_call_target="tpu_custom_call" | custom-call | tf_op jit(solution)/shard_map/mgrit_cycle/pallas_call | solution.py:556
  66.7 1.0 %write_out.1 = (f32[32,4096]{1,0:T(8,128)}, f32[32,4096]{1,0:T(8,128)}, f32[8,32,32]{2,1,0:T(8,128)}, f32[8,32]{1,0:T(8,128)}) custom-call(f32[32,4096]{1,0:T(8,128)S(1)} %get-tuple-element.12.refs_0_, f32[32,4096]{1,0:T(8,128)S(1)} %get-tuple-element.13.refs_1_, f32[8,32,32]{2,1,0:T(8,128)S(1)} %get-tuple-element.14.refs_2_, ...), custom_call_target="tpu_custom_call" | custom-call | tf_op jit(solution)/shard_map/write_out/pallas_call | solution.py:590

commit v5 on v4

--- a/solution.py
+++ b/solution.py
@@ -71,7 +71,7 @@
 def kernel(
     guess_ref, adj_ref, w_hbm, b_hbm, d_hbm, n_hbm,
     s_out, a_out, gw_out, gb_out,
-    A, T, G, LR, PUSH, LSEND, S, S2, TAU, TAU_A,
+    A, T, H, G, LR, LSEND, S, S2, TAU, TAU_A,
     WC, WT, BB, FD, WP, BP, SPA, SPAT, SPB, SPBT, CB, GB, GR,
     push_s, push_r, lam_s, lam_r, tau_s, tau_r, par_s, par_r, one_s, two_s, st_r, grad_s, grad_r,
     w_ref, b_ref, d_ref, n_ref, in_s, guess_s, adj_s, spare_s,
@@ -79,13 +79,15 @@
     sections, images = lax.axis_size("depth"), lax.axis_size("batch")
     d, image = lax.axis_index("depth"), lax.axis_index("batch")
     chunks = guess_ref.shape[1] // LANES
-    NB = min(16, chunks)
-    blocks = chunks // NB
+    blocks = 2
+    NB = chunks // blocks
+    halo = MOST // 2
     core, chip, chips = d % 2, d // 2, sections // 2
     has_prev, has_next = d > 0, d < sections - 1
     even = core == 0
     odd = core == 1
-    early, middle = (3 * chips) // 16, chips // 2
+    early = (3 * chips) // 16
+    ahead = jnp.where(even, MOST, jnp.where(chip >= (12 * chips) // 16, MOST, jnp.clip(2 * (chip - (9 * chips) // 16) - 1, 0, MOST)))
     masks = lane_masks()
     eye = lax.broadcasted_iota(jnp.int32, (C, C), 0) == lax.broadcasted_iota(jnp.int32, (C, C), 1)
 
@@ -103,7 +105,7 @@
         return pltpu.make_async_copy(src, dst, sem)
 
     def guess_in(c):
-        return brought(guess_ref.at[:, at(c)], G.at[0, c + 1], guess_s.at[c])
+        return brought(guess_ref.at[:, at(c)], H.at[0, c + 1], guess_s.at[c])
 
     def guess_start(c):
         return brought(guess_ref.at[:, at(c)], A.at[0, c + 1], spare_s.at[c])
@@ -128,6 +130,8 @@
         part.start()
     for c in range(chunks):
         guess_in(c).start()
+    for c in range(chunks):
+        adj_in(c).start()
 
     barrier = pltpu.get_barrier_semaphore()
 
@@ -162,8 +166,9 @@
 
     zero_chunk = jnp.zeros((C, LANES), F)
     for l in range(MOST + 1):
-        A[l, 0] = zero_chunk
-        A[l, chunks + 1] = zero_chunk
+        for ref in (A, H):
+            ref[l, 0] = zero_chunk
+            ref[l, chunks + 1] = zero_chunk
     for ref in (G.at[0], G.at[1], LR):
         ref[0] = zero_chunk
         ref[chunks + 1] = zero_chunk
@@ -186,52 +191,47 @@
     for c in range(chunks):
         guess_in(c).wait()
 
-    def forward_block(src, i, j, store, keep):
-        u = [src[j * NB + k] for k in range(NB + 2)]
-        laps = chunk_laps(u, NB, masks)
-        bias = jnp.concatenate([BB[i]] * NB, axis=1)
+    def forward_tile(src, i, lo, count, dst, keep, open_end):
+        u = [src[lo + k] for k in range(count + 1)] + [zero_chunk if open_end else src[lo + count + 1]]
+        laps = chunk_laps(u, count, masks)
+        bias = jnp.concatenate([BB[i]] * count, axis=1)
         act = jnp.tanh(dot3(WC[i], jnp.concatenate(u[1:-1], axis=1)) + bias)
         mixed = dot3(WT[i], act)
         fd = FD[i]
-        for k in range(NB):
-            store(j * NB + k, u[k + 1] + fd * laps[k] - mixed[:, k * LANES : (k + 1) * LANES])
+        for k in range(count):
+            dst[lo + k + 1] = u[k + 1] + fd * laps[k] - mixed[:, k * LANES : (k + 1) * LANES]
             if keep is not None:
-                keep[j * NB + k] = act[:, k * LANES : (k + 1) * LANES]
+                keep[lo + k] = act[:, k * LANES : (k + 1) * LANES]
 
     def into(ref, shift):
         def store(c, value):
             ref[c + shift] = value
         return store
 
-    def forward_layer(src, i, store, keep=None, unroll=True):
-        def block(j, _):
-            forward_block(src, i, j, store, keep)
-            return 0
-        lax.fori_loop(0, blocks, block, 0, unroll=unroll)
-
-    def first_pass(i, _):
-        forward_layer(G.at[i % 2], i, into(G.at[(i + 1) % 2], 1))
-        return 0
-
-    lax.fori_loop(0, MOST - 1, first_pass, 0)
+    def sweep(stack, keeps, lo, count, open_end):
+        def layer(i, _):
+            keep = None if keeps is None else keeps.at[i]
+            forward_tile(stack.at[i], i, lo, count, stack.at[i + 1], keep, open_end)
+            return 0
+        lax.fori_loop(0, MOST, layer, 0)
+
+    upper = NB + halo
+
+    def push_copy(j):
+        part = pl.ds(1, upper) if j == 0 else pl.ds(1 + upper, chunks - upper)
+        return copy(H.at[MOST, part], A.at[0, part], push_s.at[j], push_r.at[j], d + 1)
+
+    def push(j):
+        @pl.when(has_next)
+        def _():
+            push_copy(j).start()
+
+    first = min(upper + halo, chunks)
+    sweep(H, None, 0, first, first < chunks)
     pl.semaphore_wait(barrier, partners)
-
-    def push_copy(j):
-        return copy(
-            PUSH.at[pl.ds(j * NB, NB)], A.at[0, pl.ds(1 + j * NB, NB)], push_s.at[j], push_r.at[j], d + 1
-        )
-
-    def push_block(j, _):
-        forward_block(G.at[(MOST - 1) % 2], MOST - 1, j, into(PUSH, 0), None)
-
-        @pl.when(has_next)
-        def _():
-            push_copy(j).start()
-        return 0
-
-    lax.fori_loop(0, blocks, push_block, 0)
-    for c in range(chunks):
-        adj_in(c).start()
+    push(0)
+    sweep(H, None, upper, chunks - upper, False)
+    push(1)
 
     weight_copy = copy(w_ref.at[0], WP, par_s.at[0], par_r.at[0], d + 1)
     bias_copy = copy(b_ref, BP, par_s.at[1], par_r.at[1], d + 1)
@@ -266,21 +266,6 @@
         CB[0] = jnp.broadcast_to(column_of(BP[0:1, :], eye), (C, LANES))
         CB[1] = diff * coarse_a
 
-    @pl.when(has_prev)
-    def _():
-        for j in range(blocks):
-            push_copy(j).wait_recv()
-
-    @pl.when(starts)
-    def _():
-        each_chunk(lambda c: guess_start(c).wait())
-
-    def second_pass(i, _):
-        forward_layer(A.at[i], i, into(A.at[i + 1], 1), T.at[i])
-        return 0
-
-    lax.fori_loop(0, MOST, second_pass, 0)
-
     layers = n.astype(F)
 
     def tau_of(c):
@@ -288,25 +273,38 @@
         return A[MOST, c + 1] - (start + layers * (A[1, c + 1] - start))
 
     def tau_copy(j):
-        part = pl.ds(j * NB, NB) if j < blocks else pl.ds(chunks, 1)
+        part = pl.ds(0, NB) if j == 0 else pl.ds(NB, chunks + 1 - NB)
         return copy(TAU.at[part], TAU_A.at[part], tau_s.at[j], tau_r.at[j], d + 1)
 
-    @pl.when(even)
-    def _():
-        before = zero_chunk
-        for c in range(chunks):
-            here = tau_of(c)
-            TAU[c] = jnp.where(masks[0], here, before)
-            before = here
-            if c % NB == NB - 1:
-                tau_copy(c // NB).start()
-        TAU[chunks] = jnp.where(masks[0], 0.0, before)
-        tau_copy(blocks).start()
-
-    @pl.when(odd)
-    def _():
-        for c in range(chunks):
-            TAU[c] = tau_of(c)
+    @pl.when(starts)
+    def _():
+        each_chunk(lambda c: guess_start(c).wait())
+
+    for j in range(blocks):
+        @pl.when(has_prev)
+        def _():
+            push_copy(j).wait_recv()
+
+        if j == 0:
+            sweep(A, T, 0, upper, True)
+        else:
+            sweep(A, T, NB, chunks - NB, False)
+
+        @pl.when(even)
+        def _():
+            before = zero_chunk if j == 0 else tau_of(NB - 1)
+            for c in range(j * NB, (j + 1) * NB):
+                here = tau_of(c)
+                TAU[c] = jnp.where(masks[0], here, before)
+                before = here
+            if j == blocks - 1:
+                TAU[chunks] = jnp.where(masks[0], 0.0, before)
+            tau_copy(j).start()
+
+        @pl.when(odd)
+        def _():
+            for c in range(j * NB, (j + 1) * NB):
+                TAU[c] = tau_of(c)
 
     def one_copy(c):
         return copy(S.at[c], S.at[c], one_s.at[c], st_r.at[c], d - 1)
@@ -350,7 +348,6 @@
             if j:
                 tau_copy(j).wait_recv()
             carry = lax.fori_loop(max(1, j * NB), (j + 1) * NB, step, carry)
-        tau_copy(blocks).wait_recv()
         step(chunks, carry, last=True)
 
     def backward_block(src, i, j, store, with_grads):
@@ -407,7 +404,7 @@
 
         lax.fori_loop(0, blocks, block, 0)
 
-    def backward_full():
+    def full_ready():
         @pl.when(has_next)
         def _():
             for j in range(blocks):
@@ -421,6 +418,7 @@
             G[0, c + 1] = LR[c + 1]
         GB[MOST] = jnp.zeros((C, C), F)
 
+    def full_layers(first_layer, end_layer):
         def layer(i, _):
             slot = MOST - 1 - i
             factor = jnp.where(slot < n, 1.0 / MOST, 0.0)
@@ -435,21 +433,13 @@
             GB[MOST, pl.ds(slot, 1), :] = -factor * row_of(column, eye)
             return 0
 
-        lax.fori_loop(0, MOST, layer, 0)
-        for c in range(chunks):
-            a_out[:, c * LANES : (c + 1) * LANES] = G[0, c + 1]
-        GR[image] = GB[...]
-        for o in range(1, images):
-            grad_copy(o).start()
+        lax.fori_loop(first_layer, end_layer, layer, 0)
 
     def grad_copy(o):
         return copy(GB, GR.at[image], grad_s.at[o - 1], grad_r.at[o - 1], d, (image + o) % images)
 
     def turn(order, _):
-        relay_at = jnp.where(chip < early, 0, jnp.where(chip < middle, 1, 2))
-        start_at = jnp.where(jnp.logical_and(odd, chip < early), 1, 0)
-        full_at = jnp.where(jnp.logical_and(odd, chip >= middle), 1, 2)
-        here = jnp.logical_and(odd, order == relay_at)
+        here = jnp.logical_and(odd, order == jnp.where(chip < early, 0, 3))
 
         @pl.when(jnp.logical_and(here, chip < chips - 1))
         def _():
@@ -459,17 +449,25 @@
         def _():
             relay(False)
 
-        @pl.when(order == start_at)
+        @pl.when(order == 1)
         def _():
             backward_start()
 
-        @pl.when(order == full_at)
-        def _():
-            backward_full()
+        @pl.when(order == jnp.where(ahead > 0, 2, 4))
+        def _():
+            full_ready()
+
+        @pl.when(jnp.logical_or(order == 2, order == 4))
+        def _():
+            full_layers(jnp.where(order == 2, 0, ahead), jnp.where(order == 2, ahead, MOST))
         return 0
 
-    lax.fori_loop(0, 3, turn, 0)
-
+    lax.fori_loop(0, 5, turn, 0)
+    GR[image] = GB[...]
+    for o in range(1, images):
+        grad_copy(o).start()
+    for c in range(chunks):
+        a_out[:, c * LANES : (c + 1) * LANES] = G[0, c + 1]
     for o in range(1, images):
         grad_copy(o).wait_recv()
     for i in range(MOST + 1):
@@ -506,7 +504,7 @@
     def _():
         weight_copy.wait_send()
         bias_copy.wait_send()
-        for j in range(blocks + 1):
+        for j in range(blocks):
             tau_copy(j).wait_send()
 
     @pl.when(starts)
@@ -544,8 +542,7 @@
     pixels = cpoint_guess.shape[-1]
     images = lax.axis_size("batch")
     chunks = pixels // LANES
-    NB = min(16, chunks)
-    blocks = chunks // NB
+    blocks = 2
     vmem = pl.BlockSpec(memory_space=pltpu.VMEM)
     image_shape = jax.ShapeDtypeStruct((C, pixels), F)
     dma = pltpu.SemaphoreType.DMA
@@ -562,20 +559,20 @@
         in_specs=[pl.BlockSpec(memory_space=pltpu.HBM)] * 6,
         out_specs=(vmem,) * 4,
         scratch_shapes=[
-            stack(MOST + 1, chunks + 2), stack(MOST, chunks), stack(2, chunks + 2), stack(chunks + 2),
-            stack(chunks), stack(chunks), stack(chunks), stack(chunks), stack(chunks + 1), stack(chunks + 1),
+            stack(MOST + 1, chunks + 2), stack(MOST, chunks), stack(MOST + 1, chunks + 2), stack(2, chunks + 2),
+            stack(chunks + 2), stack(chunks), stack(chunks), stack(chunks), stack(chunks + 1), stack(chunks + 1),
             pltpu.VMEM((MOST, C, 3 * C), BF), pltpu.VMEM((MOST, C, 3 * C), BF), stack(MOST), stack(MOST),
             pltpu.VMEM((C, C), F), pltpu.VMEM((MOST, C), F),
             stack(C), stack(C), stack(C), stack(C), stack(4),
             pltpu.VMEM((MOST + 1, C, C), F), pltpu.VMEM((images, MOST + 1, C, C), F),
-            dma((blocks,)), dma((blocks,)), dma((blocks,)), dma((blocks,)), dma((blocks + 1,)), dma((blocks + 1,)),
+            dma((blocks,)), dma((blocks,)), dma((blocks,)), dma((blocks,)), dma((blocks,)), dma((blocks,)),
             dma((2,)), dma((2,)), dma((chunks,)), dma((chunks,)), dma((chunks,)),
             dma((images - 1,)), dma((images - 1,)),
             pltpu.VMEM((MOST, C, C), F), pltpu.VMEM((MOST, C), F), pltpu.VMEM((1, C), F),
             pltpu.SMEM(section_len.shape, jnp.int32), dma((4,)), dma((chunks,)), dma((chunks,)), dma((chunks,)),
         ],
         compiler_params=pltpu.CompilerParams(
-            collective_id=0, has_side_effects=True, vmem_limit_bytes=24 << 20
+            collective_id=0, has_side_effects=True, vmem_limit_bytes=32 << 20
         ),
         name="mgrit_cycle",
     )(

time: 67.9 us -> 69.6 us (1.025)
  Pallas kernels: 67.1 us -> 68.8 us
    pallas_call x1, Pallas kernels: 66.1 us -> 67.7 us  [body(): pl.pallas_call(kernel, out_shape=(image_shape, image_shape, jax.ShapeDtyp...]
where the time goes in v5:
time: 69.6 us; the launch traced here: 69.4 us
  Pallas kernels  68.8 us (99%)
    pallas_call x1, Pallas kernels, body(): pl.pallas_call(kernel, out_shape=(image_shape, image_shape, jax.ShapeDtyp...  67.7 us

profile of v5, /device:TPU:103, one launch (start us, length us, event | category | flops | bytes accessed | tf_op | source)
XLA Modules:
  0.0 69.4 jit_solution(11933629796536243437)
XLA Ops:
  0.6 67.7 %mgrit_cycle.1 = (f32[32,4096]{1,0:T(8,128)S(1)}, f32[32,4096]{1,0:T(8,128)S(1)}, f32[8,32,32]{2,1,0:T(8,128)S(1)}, f32[8,32]{1,0:T(8,128)S(1)}) custom-call(f32[32,4096]{1,0:T(8,128)} %bitcast.5, f32[32,4096]{1,0:T(8,128)} %bitcast.6, f32[8,32,32]{2,1,0:T(8,128)} %w_hbm.1, f32[8,32]{1,0:T(8,128)} %b_hbm.1, f32[1,32]{1,0:T(1,128)} %bitcast.7, s32[32]{0:T(128)} %n_hbm.1), custom_call_target="tpu_custom_call" | custom-call | tf_op jit(solution)/shard_map/mgrit_cycle/pallas_call | solution.py:553
  68.4 1.0 %write_out.1 = (f32[32,4096]{1,0:T(8,128)}, f32[32,4096]{1,0:T(8,128)}, f32[8,32,32]{2,1,0:T(8,128)}, f32[8,32]{1,0:T(8,128)}) custom-call(f32[32,4096]{1,0:T(8,128)S(1)} %get-tuple-element.12.refs_0_, f32[32,4096]{1,0:T(8,128)S(1)} %get-tuple-element.13.refs_1_, f32[8,32,32]{2,1,0:T(8,128)S(1)} %get-tuple-element.14.refs_2_, ...), custom_call_target="tpu_custom_call" | custom-call | tf_op jit(solution)/shard_map/write_out/pallas_call | solution.py:587

commit v6 on v5

--- a/solution.py
+++ b/solution.py
@@ -72,7 +72,7 @@
     guess_ref, adj_ref, w_hbm, b_hbm, d_hbm, n_hbm,
     s_out, a_out, gw_out, gb_out,
     A, T, H, G, LR, LSEND, S, S2, TAU, TAU_A,
-    WC, WT, BB, FD, WP, BP, SPA, SPAT, SPB, SPBT, CB, GB, GR,
+    WC, WT, BB, FD, WP, BP, SPA, SPAT, SPB, SPBT, CB, GB, PK, GR,
     push_s, push_r, lam_s, lam_r, tau_s, tau_r, par_s, par_r, one_s, two_s, st_r, grad_s, grad_r,
     w_ref, b_ref, d_ref, n_ref, in_s, guess_s, adj_s, spare_s,
 ):
@@ -417,6 +417,7 @@
         for c in range(chunks):
             G[0, c + 1] = LR[c + 1]
         GB[MOST] = jnp.zeros((C, C), F)
+        PK[...] = jnp.zeros_like(PK)
 
     def full_layers(first_layer, end_layer):
         def layer(i, _):
@@ -435,8 +436,20 @@
 
         lax.fori_loop(first_layer, end_layer, layer, 0)
 
+    side = LANES // C
+
+    def share_grads():
+        for g in range(MOST // side):
+            PK[g * C : (g + 1) * C] = jnp.concatenate([GB[g * side + k] for k in range(side)], axis=1)
+        PK[MOST // side * C :, :C] = GB[MOST, :MOST]
+        GR[image] = PK[...]
+        for o in range(1, images):
+            grad_copy(o).start()
+        for c in range(chunks):
+            a_out[:, c * LANES : (c + 1) * LANES] = G[0, c + 1]
+
     def grad_copy(o):
-        return copy(GB, GR.at[image], grad_s.at[o - 1], grad_r.at[o - 1], d, (image + o) % images)
+        return copy(PK, GR.at[image], grad_s.at[o - 1], grad_r.at[o - 1], d, (image + o) % images)
 
     def turn(order, _):
         here = jnp.logical_and(odd, order == jnp.where(chip < early, 0, 3))
@@ -460,24 +473,22 @@
         @pl.when(jnp.logical_or(order == 2, order == 4))
         def _():
             full_layers(jnp.where(order == 2, 0, ahead), jnp.where(order == 2, ahead, MOST))
+
+        @pl.when(order == jnp.where(ahead == MOST, 2, 4))
+        def _():
+            share_grads()
         return 0
 
     lax.fori_loop(0, 5, turn, 0)
-    GR[image] = GB[...]
-    for o in range(1, images):
-        grad_copy(o).start()
-    for c in range(chunks):
-        a_out[:, c * LANES : (c + 1) * LANES] = G[0, c + 1]
     for o in range(1, images):
         grad_copy(o).wait_recv()
-    for i in range(MOST + 1):
-        total = GR[0, i]
-        for b in range(1, images):
-            total = total + GR[b, i]
-        if i < MOST:
-            gw_out[i] = total
-        else:
-            gb_out[...] = total[:MOST]
+    total = GR[0]
+    for b in range(1, images):
+        total = total + GR[b]
+    for i in range(MOST):
+        row, lane = i // side * C, i % side * C
+        gw_out[i] = total[row : row + C, lane : lane + C]
+    gb_out[...] = total[MOST // side * C :, :C]
 
     @pl.when(even)
     def _():
@@ -564,7 +575,8 @@
             pltpu.VMEM((MOST, C, 3 * C), BF), pltpu.VMEM((MOST, C, 3 * C), BF), stack(MOST), stack(MOST),
             pltpu.VMEM((C, C), F), pltpu.VMEM((MOST, C), F),
             stack(C), stack(C), stack(C), stack(C), stack(4),
-            pltpu.VMEM((MOST + 1, C, C), F), pltpu.VMEM((images, MOST + 1, C, C), F),
+            pltpu.VMEM((MOST + 1, C, C), F),
+            pltpu.VMEM((MOST // 4 * C + MOST, LANES), F), pltpu.VMEM((images, MOST // 4 * C + MOST, LANES), F),
             dma((blocks,)), dma((blocks,)), dma((blocks,)), dma((blocks,)), dma((blocks,)), dma((blocks,)),
             dma((2,)), dma((2,)), dma((chunks,)), dma((chunks,)), dma((chunks,)),
             dma((images - 1,)), dma((images - 1,)),

time: 69.6 us -> 63.3 us (0.909); the launches traced: 69.4 us -> 62.3 us
  Pallas kernels: 68.8 us -> 61.6 us
    pallas_call x1, Pallas kernels: 67.7 us -> 60.6 us  [body(): pl.pallas_call(kernel, out_shape=(image_shape, image_shape, jax.ShapeDtyp...]
where the time goes in v6:
time: 63.3 us; the launch traced here: 62.3 us
  Pallas kernels  61.6 us (97%)
  between operations  0.64 us (1%)
    pallas_call x1, Pallas kernels, body(): pl.pallas_call(kernel, out_shape=(image_shape, image_shape, jax.ShapeDtyp...  60.6 us

profile of v6, /device:TPU:103, one launch (start us, length us, event | category | flops | bytes accessed | tf_op | source)
XLA Modules:
  0.0 62.3 jit_solution(13244021483305276971)
XLA Ops:
  0.6 60.6 %mgrit_cycle.1 = (f32[32,4096]{1,0:T(8,128)S(1)}, f32[32,4096]{1,0:T(8,128)S(1)}, f32[8,32,32]{2,1,0:T(8,128)S(1)}, f32[8,32]{1,0:T(8,128)S(1)}) custom-call(f32[32,4096]{1,0:T(8,128)} %bitcast.5, f32[32,4096]{1,0:T(8,128)} %bitcast.6, f32[8,32,32]{2,1,0:T(8,128)} %w_hbm.1, f32[8,32]{1,0:T(8,128)} %b_hbm.1, f32[1,32]{1,0:T(1,128)} %bitcast.7, s32[32]{0:T(128)} %n_hbm.1), custom_call_target="tpu_custom_call" | custom-call | tf_op jit(solution)/shard_map/mgrit_cycle/pallas_call | solution.py:564
  61.2 1.0 %write_out.1 = (f32[32,4096]{1,0:T(8,128)}, f32[32,4096]{1,0:T(8,128)}, f32[8,32,32]{2,1,0:T(8,128)}, f32[8,32]{1,0:T(8,128)}) custom-call(f32[32,4096]{1,0:T(8,128)S(1)} %get-tuple-element.12.refs_0_, f32[32,4096]{1,0:T(8,128)S(1)} %get-tuple-element.13.refs_1_, f32[8,32,32]{2,1,0:T(8,128)S(1)} %get-tuple-element.14.refs_2_, ...), custom_call_target="tpu_custom_call" | custom-call | tf_op jit(solution)/shard_map/write_out/pallas_call | solution.py:599

commit v7 on v6

--- a/solution.py
+++ b/solution.py
@@ -69,12 +69,12 @@
 
 
 def kernel(
-    guess_ref, adj_ref, w_hbm, b_hbm, d_hbm, n_hbm,
+    guess_hbm, adj_hbm, w_hbm, b_hbm, d_hbm, n_hbm,
     s_out, a_out, gw_out, gb_out,
     A, T, H, G, LR, LSEND, S, S2, TAU, TAU_A,
     WC, WT, BB, FD, WP, BP, SPA, SPAT, SPB, SPBT, CB, GB, PK, GR,
-    push_s, push_r, lam_s, lam_r, tau_s, tau_r, par_s, par_r, one_s, two_s, st_r, grad_s, grad_r,
-    w_ref, b_ref, d_ref, n_ref, in_s, guess_s, adj_s, spare_s,
+    push_s, push_r, lam_s, lam_r, tau_s, tau_r, par_s, par_r, one_s, one_r, two_s, st_r, grad_s, grad_r,
+    guess_ref, adj_ref, w_ref, b_ref, d_ref, n_ref, in_s,
 ):
     sections, images = lax.axis_size("depth"), lax.axis_size("batch")
     d, image = lax.axis_index("depth"), lax.axis_index("batch")
@@ -82,12 +82,14 @@
     blocks = 2
     NB = chunks // blocks
     halo = MOST // 2
+    cut = (3 * chunks) // 8
+    parts = ((0, cut), (cut, chunks))
     core, chip, chips = d % 2, d // 2, sections // 2
     has_prev, has_next = d > 0, d < sections - 1
     even = core == 0
     odd = core == 1
-    early = (3 * chips) // 16
-    ahead = jnp.where(even, MOST, jnp.where(chip >= (12 * chips) // 16, MOST, jnp.clip(2 * (chip - (9 * chips) // 16) - 1, 0, MOST)))
+    early = chips // 4
+    ahead = jnp.where(even, MOST, jnp.where(chip >= (12 * chips) // 16, MOST, jnp.clip(2 * (chip - (9 * chips) // 16), 0, MOST)))
     masks = lane_masks()
     eye = lax.broadcasted_iota(jnp.int32, (C, C), 0) == lax.broadcasted_iota(jnp.int32, (C, C), 1)
 
@@ -104,34 +106,15 @@
     def brought(src, dst, sem):
         return pltpu.make_async_copy(src, dst, sem)
 
-    def guess_in(c):
-        return brought(guess_ref.at[:, at(c)], H.at[0, c + 1], guess_s.at[c])
-
-    def guess_start(c):
-        return brought(guess_ref.at[:, at(c)], A.at[0, c + 1], spare_s.at[c])
-
-    def adj_in(c):
-        return brought(adj_ref.at[:, at(c)], G.at[0, c + 1], adj_s.at[c])
-
-    def adj_end(c):
-        return brought(adj_ref.at[:, at(c)], LR.at[c + 1], spare_s.at[c])
-
-    def each_chunk(action):
-        def one(c, _):
-            action(c)
-            return 0
-        lax.fori_loop(0, chunks, one, 0)
-
     small = [
         brought(src, dst, in_s.at[i])
         for i, (src, dst) in enumerate(((n_hbm, n_ref), (w_hbm, w_ref), (b_hbm, b_ref), (d_hbm, d_ref)))
     ]
+    guess_in, adj_in = brought(guess_hbm, guess_ref, in_s.at[4]), brought(adj_hbm, adj_ref, in_s.at[5])
     for part in small:
         part.start()
-    for c in range(chunks):
-        guess_in(c).start()
-    for c in range(chunks):
-        adj_in(c).start()
+    guess_in.start()
+    adj_in.start()
 
     barrier = pltpu.get_barrier_semaphore()
 
@@ -156,14 +139,6 @@
 
     starts, ends = jnp.logical_not(has_prev), jnp.logical_not(has_next)
 
-    @pl.when(starts)
-    def _():
-        each_chunk(lambda c: guess_start(c).start())
-
-    @pl.when(ends)
-    def _():
-        each_chunk(lambda c: adj_end(c).start())
-
     zero_chunk = jnp.zeros((C, LANES), F)
     for l in range(MOST + 1):
         for ref in (A, H):
@@ -188,8 +163,9 @@
         return 0
 
     lax.fori_loop(0, MOST, prepare, 0, unroll=True)
+    guess_in.wait()
     for c in range(chunks):
-        guess_in(c).wait()
+        H[0, c + 1] = guess_ref[:, c * LANES : (c + 1) * LANES]
 
     def forward_tile(src, i, lo, count, dst, keep, open_end):
         u = [src[lo + k] for k in range(count + 1)] + [zero_chunk if open_end else src[lo + count + 1]]
@@ -215,7 +191,7 @@
             return 0
         lax.fori_loop(0, MOST, layer, 0)
 
-    upper = NB + halo
+    upper = cut + halo
 
     def push_copy(j):
         part = pl.ds(1, upper) if j == 0 else pl.ds(1 + upper, chunks - upper)
@@ -237,7 +213,7 @@
     bias_copy = copy(b_ref, BP, par_s.at[1], par_r.at[1], d + 1)
 
     def first_copy(c):
-        return copy(guess_ref.at[:, at(c)], S.at[c], one_s.at[c], st_r.at[c], d + 1)
+        return copy(guess_ref.at[:, at(c)], S.at[c], two_s.at[0], st_r.at[c], d + 1)
 
     @pl.when(even)
     def _():
@@ -273,44 +249,52 @@
         return A[MOST, c + 1] - (start + layers * (A[1, c + 1] - start))
 
     def tau_copy(j):
-        part = pl.ds(0, NB) if j == 0 else pl.ds(NB, chunks + 1 - NB)
+        part = pl.ds(0, cut) if j == 0 else pl.ds(cut, chunks + 1 - cut)
         return copy(TAU.at[part], TAU_A.at[part], tau_s.at[j], tau_r.at[j], d + 1)
 
     @pl.when(starts)
     def _():
-        each_chunk(lambda c: guess_start(c).wait())
-
-    for j in range(blocks):
+        for c in range(chunks):
+            A[0, c + 1] = guess_ref[:, c * LANES : (c + 1) * LANES]
+
+    def push_arrived(j):
         @pl.when(has_prev)
         def _():
             push_copy(j).wait_recv()
 
-        if j == 0:
-            sweep(A, T, 0, upper, True)
-        else:
-            sweep(A, T, NB, chunks - NB, False)
-
-        @pl.when(even)
-        def _():
-            before = zero_chunk if j == 0 else tau_of(NB - 1)
-            for c in range(j * NB, (j + 1) * NB):
+    @pl.when(even)
+    def _():
+        for j, (lo, hi) in enumerate(parts):
+            push_arrived(j)
+            if j == 0:
+                sweep(A, T, 0, upper, True)
+            else:
+                sweep(A, T, cut, chunks - cut, False)
+            before = zero_chunk if j == 0 else tau_of(cut - 1)
+            for c in range(lo, hi):
                 here = tau_of(c)
                 TAU[c] = jnp.where(masks[0], here, before)
                 before = here
-            if j == blocks - 1:
+            if j == 1:
                 TAU[chunks] = jnp.where(masks[0], 0.0, before)
             tau_copy(j).start()
 
-        @pl.when(odd)
-        def _():
-            for c in range(j * NB, (j + 1) * NB):
-                TAU[c] = tau_of(c)
-
-    def one_copy(c):
-        return copy(S.at[c], S.at[c], one_s.at[c], st_r.at[c], d - 1)
+    @pl.when(odd)
+    def _():
+        for j in range(2):
+            push_arrived(j)
+        sweep(A, T, 0, chunks, False)
+        for c in range(chunks):
+            TAU[c] = tau_of(c)
+
+    hand = (0, cut, chunks - chunks // 8, chunks)
+
+    def one_copy(p):
+        part = pl.ds(hand[p], hand[p + 1] - hand[p])
+        return copy(S.at[part], S.at[part], one_s.at[p], one_r.at[p], d - 1)
 
     def two_copy(c):
-        return copy(S2.at[c], S.at[c], two_s.at[c], st_r.at[c], d + 2)
+        return copy(S2.at[c], S.at[c], two_s.at[0], st_r.at[c], d + 2)
 
     def relay(both):
         bias_a, fd_a, bias_b, fd_b = CB[0], CB[1], CB[2], CB[3]
@@ -322,7 +306,6 @@
                 now = zero_chunk
             else:
                 two_copy(c).wait_recv()
-                one_copy(c).start()
                 now = S[c]
             mid = jnp.where(lower, now, prev)
             lap = (pltpu.roll(prev + now, 64, 1) + beside(mid, masks)) - 4.0 * mid
@@ -344,10 +327,11 @@
 
         tau_copy(0).wait_recv()
         carry = step(0, (zero_chunk,) * 2, first=True)
-        for j in range(blocks):
-            if j:
-                tau_copy(j).wait_recv()
-            carry = lax.fori_loop(max(1, j * NB), (j + 1) * NB, step, carry)
+        for p in range(3):
+            if p == 1:
+                tau_copy(1).wait_recv()
+            carry = lax.fori_loop(max(1, hand[p]), hand[p + 1], step, carry)
+            one_copy(p).start()
         step(chunks, carry, last=True)
 
     def backward_block(src, i, j, store, with_grads):
@@ -382,8 +366,9 @@
         return copy(LSEND.at[pl.ds(j * NB, NB)], LR.at[pl.ds(1 + j * NB, NB)], lam_s.at[j], lam_r.at[j], d - 1)
 
     def backward_start():
+        adj_in.wait()
         for c in range(chunks):
-            adj_in(c).wait()
+            G[0, c + 1] = adj_ref[:, c * LANES : (c + 1) * LANES]
 
         def layer(i, _):
             def block(j, _):
@@ -412,7 +397,8 @@
 
         @pl.when(ends)
         def _():
-            each_chunk(lambda c: adj_end(c).wait())
+            for c in range(chunks):
+                LR[c + 1] = adj_ref[:, c * LANES : (c + 1) * LANES]
 
         for c in range(chunks):
             G[0, c + 1] = LR[c + 1]
@@ -492,11 +478,10 @@
 
     @pl.when(even)
     def _():
-        def take(c, _):
-            one_copy(c).wait_recv()
-            s_out[:, at(c)] = S[c]
-            return 0
-        lax.fori_loop(0, chunks, take, 0)
+        for p in range(3):
+            one_copy(p).wait_recv()
+            for c in range(hand[p], hand[p + 1]):
+                s_out[:, c * LANES : (c + 1) * LANES] = S[c]
 
     for o in range(1, images):
         grad_copy(o).wait_send()
@@ -518,26 +503,15 @@
         for j in range(blocks):
             tau_copy(j).wait_send()
 
-    @pl.when(starts)
-    def _():
-        def sent(c, _):
-            first_copy(c).wait_send()
-            return 0
-        lax.fori_loop(0, chunks, sent, 0)
-
     @pl.when(odd)
     def _():
-        def sent(c, _):
-            one_copy(c).wait_send()
-            return 0
-        lax.fori_loop(0, chunks, sent, 0)
-
-    @pl.when(up2)
-    def _():
-        def sent(c, _):
-            two_copy(c).wait_send()
-            return 0
-        lax.fori_loop(0, chunks, sent, 0)
+        for p in range(3):
+            one_copy(p).wait_send()
+
+    @pl.when(jnp.logical_or(starts, up2))
+    def _():
+        part = pl.ds(0, chunks)
+        copy(S2.at[part], S.at[part], two_s.at[0], st_r.at[0], d + 1).wait_send()
 
 
 def write_out(*refs):
@@ -578,10 +552,11 @@
             pltpu.VMEM((MOST + 1, C, C), F),
             pltpu.VMEM((MOST // 4 * C + MOST, LANES), F), pltpu.VMEM((images, MOST // 4 * C + MOST, LANES), F),
             dma((blocks,)), dma((blocks,)), dma((blocks,)), dma((blocks,)), dma((blocks,)), dma((blocks,)),
-            dma((2,)), dma((2,)), dma((chunks,)), dma((chunks,)), dma((chunks,)),
+            dma((2,)), dma((2,)), dma((3,)), dma((3,)), dma((1,)), dma((chunks,)),
             dma((images - 1,)), dma((images - 1,)),
+            pltpu.VMEM((C, pixels), F), pltpu.VMEM((C, pixels), F),
             pltpu.VMEM((MOST, C, C), F), pltpu.VMEM((MOST, C), F), pltpu.VMEM((1, C), F),
-            pltpu.SMEM(section_len.shape, jnp.int32), dma((4,)), dma((chunks,)), dma((chunks,)), dma((chunks,)),
+            pltpu.SMEM(section_len.shape, jnp.int32), dma((6,)),
         ],
         compiler_params=pltpu.CompilerParams(
             collective_id=0, has_side_effects=True, vmem_limit_bytes=32 << 20

time: 63.3 us -> 59.2 us (0.935)
  Pallas kernels: 61.6 us -> 58.1 us
    pallas_call x1, Pallas kernels: 60.6 us -> 57 us  [body(): pl.pallas_call(kernel, out_shape=(image_shape, image_shape, jax.ShapeDtyp...]
where the time goes in v7:
time: 59.2 us; the launch traced here: 58.7 us
  Pallas kernels  58.1 us (98%)
  between operations  0.64 us (1%)
    pallas_call x1, Pallas kernels, body(): pl.pallas_call(kernel, out_shape=(image_shape, image_shape, jax.ShapeDtyp...  57 us

profile of v7, /device:TPU:103, one launch (start us, length us, event | category | flops | bytes accessed | tf_op | source)
XLA Modules:
  0.0 58.7 jit_solution(7452288051351468774)
XLA Ops:
  0.6 57.0 %mgrit_cycle.1 = (f32[32,4096]{1,0:T(8,128)S(1)}, f32[32,4096]{1,0:T(8,128)S(1)}, f32[8,32,32]{2,1,0:T(8,128)S(1)}, f32[8,32]{1,0:T(8,128)S(1)}) custom-call(f32[32,4096]{1,0:T(8,128)} %bitcast.5, f32[32,4096]{1,0:T(8,128)} %bitcast.6, f32[8,32,32]{2,1,0:T(8,128)} %w_hbm.1, f32[8,32]{1,0:T(8,128)} %b_hbm.1, f32[1,32]{1,0:T(1,128)} %bitcast.7, s32[32]{0:T(128)} %n_hbm.1), custom_call_target="tpu_custom_call" | custom-call | tf_op jit(solution)/shard_map/mgrit_cycle/pallas_call | solution.py:538
  57.7 1.0 %write_out.1 = (f32[32,4096]{1,0:T(8,128)}, f32[32,4096]{1,0:T(8,128)}, f32[8,32,32]{2,1,0:T(8,128)}, f32[8,32]{1,0:T(8,128)}) custom-call(f32[32,4096]{1,0:T(8,128)S(1)} %get-tuple-element.12.refs_0_, f32[32,4096]{1,0:T(8,128)S(1)} %get-tuple-element.13.refs_1_, f32[8,32,32]{2,1,0:T(8,128)S(1)} %get-tuple-element.14.refs_2_, ...), custom_call_target="tpu_custom_call" | custom-call | tf_op jit(solution)/shard_map/write_out/pallas_call | solution.py:574

commit v8 on v7

--- a/solution.py
+++ b/solution.py
@@ -72,7 +72,7 @@
     guess_hbm, adj_hbm, w_hbm, b_hbm, d_hbm, n_hbm,
     s_out, a_out, gw_out, gb_out,
     A, T, H, G, LR, LSEND, S, S2, TAU, TAU_A,
-    WC, WT, BB, FD, WP, BP, SPA, SPAT, SPB, SPBT, CB, GB, PK, GR,
+    WC, WT, BB, FD, SPA, SPAT, SPB, SPBT, CB, GB, PK, GR,
     push_s, push_r, lam_s, lam_r, tau_s, tau_r, par_s, par_r, one_s, one_r, two_s, st_r, grad_s, grad_r,
     guess_ref, adj_ref, w_ref, b_ref, d_ref, n_ref, in_s,
 ):
@@ -88,7 +88,7 @@
     has_prev, has_next = d > 0, d < sections - 1
     even = core == 0
     odd = core == 1
-    early = chips // 4
+    early = chips // 4 + 1
     ahead = jnp.where(even, MOST, jnp.where(chip >= (12 * chips) // 16, MOST, jnp.clip(2 * (chip - (9 * chips) // 16), 0, MOST)))
     masks = lane_masks()
     eye = lax.broadcasted_iota(jnp.int32, (C, C), 0) == lax.broadcasted_iota(jnp.int32, (C, C), 1)
@@ -187,9 +187,13 @@
     def sweep(stack, keeps, lo, count, open_end):
         def layer(i, _):
             keep = None if keeps is None else keeps.at[i]
-            forward_tile(stack.at[i], i, lo, count, stack.at[i + 1], keep, open_end)
+            forward_tile(stack.at[i], i, lo, wide, stack.at[i + 1], keep, open_end)
             return 0
-        lax.fori_loop(0, MOST, layer, 0)
+
+        wide = count
+        lax.fori_loop(0, MOST // 2, layer, 0)
+        wide = count - halo // 2 if open_end else count
+        lax.fori_loop(MOST // 2, MOST, layer, 0)
 
     upper = cut + halo
 
@@ -209,16 +213,14 @@
     sweep(H, None, upper, chunks - upper, False)
     push(1)
 
-    weight_copy = copy(w_ref.at[0], WP, par_s.at[0], par_r.at[0], d + 1)
-    bias_copy = copy(b_ref, BP, par_s.at[1], par_r.at[1], d + 1)
+    part_copies = [
+        copy(SPA, SPA, par_s.at[0], par_r.at[0], d + 1),
+        copy(SPAT, SPAT, par_s.at[1], par_r.at[1], d + 1),
+        copy(CB.at[0:2], CB.at[0:2], par_s.at[2], par_r.at[2], d + 1),
+    ]
 
     def first_copy(c):
         return copy(guess_ref.at[:, at(c)], S.at[c], two_s.at[0], st_r.at[c], d + 1)
-
-    @pl.when(even)
-    def _():
-        weight_copy.start()
-        bias_copy.start()
 
     @pl.when(starts)
     def _():
@@ -227,20 +229,23 @@
             return 0
         lax.fori_loop(0, chunks, send, 0)
 
+    def propagator(matrix_ref, back_ref, row):
+        spread(w_ref[0], matrix_ref)
+        spread(w_ref[0].T * -coarse, back_ref)
+        CB[row] = BB[0]
+        CB[row + 1] = diff * coarse
+
+    coarse = n.astype(F) / MOST
+
+    @pl.when(even)
+    def _():
+        propagator(SPA, SPAT, 0)
+        for part in part_copies:
+            part.start()
+
     @pl.when(odd)
     def _():
-        coarse_b = n.astype(F) / MOST
-        spread(w_ref[0], SPB)
-        spread(w_ref[0].T * -coarse_b, SPBT)
-        CB[2] = BB[0]
-        CB[3] = diff * coarse_b
-        weight_copy.wait_recv()
-        bias_copy.wait_recv()
-        coarse_a = n_ref[d - core].astype(F) / MOST
-        spread(WP[...], SPA)
-        spread(WP[...].T * -coarse_a, SPAT)
-        CB[0] = jnp.broadcast_to(column_of(BP[0:1, :], eye), (C, LANES))
-        CB[1] = diff * coarse_a
+        propagator(SPB, SPBT, 2)
 
     layers = n.astype(F)
 
@@ -297,6 +302,8 @@
         return copy(S2.at[c], S.at[c], two_s.at[0], st_r.at[c], d + 2)
 
     def relay(both):
+        for part in part_copies:
+            part.wait_recv()
         bias_a, fd_a, bias_b, fd_b = CB[0], CB[1], CB[2], CB[3]
         lower = masks[0]
 
@@ -498,8 +505,8 @@
 
     @pl.when(even)
     def _():
-        weight_copy.wait_send()
-        bias_copy.wait_send()
+        for part in part_copies:
+            part.wait_send()
         for j in range(blocks):
             tau_copy(j).wait_send()
 
@@ -547,12 +554,11 @@
             stack(MOST + 1, chunks + 2), stack(MOST, chunks), stack(MOST + 1, chunks + 2), stack(2, chunks + 2),
             stack(chunks + 2), stack(chunks), stack(chunks), stack(chunks), stack(chunks + 1), stack(chunks + 1),
             pltpu.VMEM((MOST, C, 3 * C), BF), pltpu.VMEM((MOST, C, 3 * C), BF), stack(MOST), stack(MOST),
-            pltpu.VMEM((C, C), F), pltpu.VMEM((MOST, C), F),
             stack(C), stack(C), stack(C), stack(C), stack(4),
             pltpu.VMEM((MOST + 1, C, C), F),
             pltpu.VMEM((MOST // 4 * C + MOST, LANES), F), pltpu.VMEM((images, MOST // 4 * C + MOST, LANES), F),
             dma((blocks,)), dma((blocks,)), dma((blocks,)), dma((blocks,)), dma((blocks,)), dma((blocks,)),
-            dma((2,)), dma((2,)), dma((3,)), dma((3,)), dma((1,)), dma((chunks,)),
+            dma((3,)), dma((3,)), dma((3,)), dma((3,)), dma((1,)), dma((chunks,)),
             dma((images - 1,)), dma((images - 1,)),
             pltpu.VMEM((C, pixels), F), pltpu.VMEM((C, pixels), F),
             pltpu.VMEM((MOST, C, C), F), pltpu.VMEM((MOST, C), F), pltpu.VMEM((1, C), F),

time: 59.2 us -> 58.8 us (level)
  no operation moved by 1% of the time
where the time goes in v8:
time: 58.8 us; the launch traced here: 58.5 us
  Pallas kernels  57.9 us (98%)
  between operations  0.64 us (1%)
    pallas_call x1, Pallas kernels, body(): pl.pallas_call(kernel, out_shape=(image_shape, image_shape, jax.ShapeDtyp...  56.8 us

profile of v8, /device:TPU:103, one launch (start us, length us, event | category | flops | bytes accessed | tf_op | source)
XLA Modules:
  0.0 58.5 jit_solution(1175244078344532530)
XLA Ops:
  0.6 56.8 %mgrit_cycle.1 = (f32[32,4096]{1,0:T(8,128)S(1)}, f32[32,4096]{1,0:T(8,128)S(1)}, f32[8,32,32]{2,1,0:T(8,128)S(1)}, f32[8,32]{1,0:T(8,128)S(1)}) custom-call(f32[32,4096]{1,0:T(8,128)} %bitcast.5, f32[32,4096]{1,0:T(8,128)} %bitcast.6, f32[8,32,32]{2,1,0:T(8,128)} %w_hbm.1, f32[8,32]{1,0:T(8,128)} %b_hbm.1, f32[1,32]{1,0:T(1,128)} %bitcast.7, s32[32]{0:T(128)} %n_hbm.1), custom_call_target="tpu_custom_call" | custom-call | tf_op jit(solution)/shard_map/mgrit_cycle/pallas_call | solution.py:545
  57.5 1.0 %write_out.1 = (f32[32,4096]{1,0:T(8,128)}, f32[32,4096]{1,0:T(8,128)}, f32[8,32,32]{2,1,0:T(8,128)}, f32[8,32]{1,0:T(8,128)}) custom-call(f32[32,4096]{1,0:T(8,128)S(1)} %get-tuple-element.12.refs_0_, f32[32,4096]{1,0:T(8,128)S(1)} %get-tuple-element.13.refs_1_, f32[8,32,32]{2,1,0:T(8,128)S(1)} %get-tuple-element.14.refs_2_, ...), custom_call_target="tpu_custom_call" | custom-call | tf_op jit(solution)/shard_map/write_out/pallas_call | solution.py:580

commit v9 on v8

--- a/solution.py
+++ b/solution.py
@@ -304,11 +304,21 @@
     def relay(both):
         for part in part_copies:
             part.wait_recv()
+        lower = masks[0]
         bias_a, fd_a, bias_b, fd_b = CB[0], CB[1], CB[2], CB[3]
-        lower = masks[0]
+        bias_ab, bias_ba = jnp.where(lower, bias_a, bias_b), jnp.where(lower, bias_b, bias_a)
+
+        for k in range(C):
+            for first_ref, second_ref in ((SPA, SPB), (SPAT, SPBT)):
+                one, two = first_ref[k], second_ref[k]
+                first_ref[k] = jnp.where(lower, one, two)
+                second_ref[k] = jnp.where(lower, two, one)
+
+        def pull(there_ref, back_ref, x, bias):
+            return mix(back_ref, jnp.tanh(mix(there_ref, x, bias)), None)
 
         def step(c, carry, first=False, last=False):
-            prev, one_prev = carry
+            prev, one_prev, ready = carry
             if last:
                 now = zero_chunk
             else:
@@ -316,8 +326,9 @@
                 now = S[c]
             mid = jnp.where(lower, now, prev)
             lap = (pltpu.roll(prev + now, 64, 1) + beside(mid, masks)) - 4.0 * mid
-            act = jnp.tanh(mix(SPA, mid, bias_a))
-            one = mix(SPAT, act, mid + fd_a * lap + TAU_A[c])
+            base = mid + fd_a * lap + TAU_A[c]
+            pulled = pull(SPA, SPAT, jnp.where(lower, now, base + ready), bias_ab)
+            one = base + jnp.where(lower, pulled, ready)
             if first:
                 one = jnp.where(lower, one, 0.0)
             if last:
@@ -326,14 +337,15 @@
                 mid_one = jnp.where(lower, one_prev, one)
                 if both:
                     lap_b = (pltpu.roll(one_prev + one, 64, 1) + beside(mid_one, masks)) - 4.0 * mid_one
-                    act_b = jnp.tanh(mix(SPB, mid_one, bias_b))
-                    S2[c - 1] = mix(SPBT, act_b, mid_one + fd_b * lap_b + TAU[c - 1])
+                    S2[c - 1] = (mid_one + fd_b * lap_b + TAU[c - 1]) + jnp.where(lower, ready, pulled)
                     two_copy(c - 1).start()
                 s_out[:, at(c - 1)] = mid_one
-            return now, one
+            if last:
+                return None
+            return now, one, pull(SPB, SPBT, jnp.where(lower, one, now), bias_ba)
 
         tau_copy(0).wait_recv()
-        carry = step(0, (zero_chunk,) * 2, first=True)
+        carry = step(0, (zero_chunk,) * 3, first=True)
         for p in range(3):
             if p == 1:
                 tau_copy(1).wait_recv()

time: 58.8 us -> 64.9 us (1.10)
  Pallas kernels: 57.9 us -> 64 us
    pallas_call x1, Pallas kernels: 56.8 us -> 62.9 us  [body(): pl.pallas_call(kernel, out_shape=(image_shape, image_shape, jax.ShapeDtyp...]
where the time goes in v9:
time: 64.9 us; the launch traced here: 64.6 us
  Pallas kernels  64 us (99%)
    pallas_call x1, Pallas kernels, body(): pl.pallas_call(kernel, out_shape=(image_shape, image_shape, jax.ShapeDtyp...  62.9 us

profile of v9, /device:TPU:103, one launch (start us, length us, event | category | flops | bytes accessed | tf_op | source)
XLA Modules:
  0.0 64.6 jit_solution(5429828228028844145)
XLA Ops:
  0.6 62.9 %mgrit_cycle.1 = (f32[32,4096]{1,0:T(8,128)S(1)}, f32[32,4096]{1,0:T(8,128)S(1)}, f32[8,32,32]{2,1,0:T(8,128)S(1)}, f32[8,32]{1,0:T(8,128)S(1)}) custom-call(f32[32,4096]{1,0:T(8,128)} %bitcast.5, f32[32,4096]{1,0:T(8,128)} %bitcast.6, f32[8,32,32]{2,1,0:T(8,128)} %w_hbm.1, f32[8,32]{1,0:T(8,128)} %b_hbm.1, f32[1,32]{1,0:T(1,128)} %bitcast.7, s32[32]{0:T(128)} %n_hbm.1), custom_call_target="tpu_custom_call" | custom-call | tf_op jit(solution)/shard_map/mgrit_cycle/pallas_call | solution.py:557
  63.6 1.0 %write_out.1 = (f32[32,4096]{1,0:T(8,128)}, f32[32,4096]{1,0:T(8,128)}, f32[8,32,32]{2,1,0:T(8,128)}, f32[8,32]{1,0:T(8,128)}) custom-call(f32[32,4096]{1,0:T(8,128)S(1)} %get-tuple-element.12.refs_0_, f32[32,4096]{1,0:T(8,128)S(1)} %get-tuple-element.13.refs_1_, f32[8,32,32]{2,1,0:T(8,128)S(1)} %get-tuple-element.14.refs_2_, ...), custom_call_target="tpu_custom_call" | custom-call | tf_op jit(solution)/shard_map/write_out/pallas_call | solution.py:592

commit v10 on v8

--- a/solution.py
+++ b/solution.py
@@ -337,7 +337,9 @@
         for p in range(3):
             if p == 1:
                 tau_copy(1).wait_recv()
-            carry = lax.fori_loop(max(1, hand[p]), hand[p + 1], step, carry)
+            if p == 0:
+                carry = step(1, carry)
+            carry = lax.fori_loop(max(2, hand[p]), hand[p + 1], step, carry, unroll=2)
             one_copy(p).start()
         step(chunks, carry, last=True)
 

time: 58.8 us -> 58.9 us (level)
  no operation moved by 1% of the time
where the time goes in v10:
time: 58.9 us; the launch traced here: 58.7 us
  Pallas kernels  58 us (98%)
  between operations  0.64 us (1%)
    pallas_call x1, Pallas kernels, body(): pl.pallas_call(kernel, out_shape=(image_shape, image_shape, jax.ShapeDtyp...  57 us

profile of v10, /device:TPU:103, one launch (start us, length us, event | category | flops | bytes accessed | tf_op | source)
XLA Modules:
  0.0 58.7 jit_solution(12611174852022700819)
XLA Ops:
  0.6 57.0 %mgrit_cycle.1 = (f32[32,4096]{1,0:T(8,128)S(1)}, f32[32,4096]{1,0:T(8,128)S(1)}, f32[8,32,32]{2,1,0:T(8,128)S(1)}, f32[8,32]{1,0:T(8,128)S(1)}) custom-call(f32[32,4096]{1,0:T(8,128)} %bitcast.5, f32[32,4096]{1,0:T(8,128)} %bitcast.6, f32[8,32,32]{2,1,0:T(8,128)} %w_hbm.1, f32[8,32]{1,0:T(8,128)} %b_hbm.1, f32[1,32]{1,0:T(1,128)} %bitcast.7, s32[32]{0:T(128)} %n_hbm.1), custom_call_target="tpu_custom_call" | custom-call | tf_op jit(solution)/shard_map/mgrit_cycle/pallas_call | solution.py:547
  57.6 1.0 %write_out.1 = (f32[32,4096]{1,0:T(8,128)}, f32[32,4096]{1,0:T(8,128)}, f32[8,32,32]{2,1,0:T(8,128)}, f32[8,32]{1,0:T(8,128)}) custom-call(f32[32,4096]{1,0:T(8,128)S(1)} %get-tuple-element.12.refs_0_, f32[32,4096]{1,0:T(8,128)S(1)} %get-tuple-element.13.refs_1_, f32[8,32,32]{2,1,0:T(8,128)S(1)} %get-tuple-element.14.refs_2_, ...), custom_call_target="tpu_custom_call" | custom-call | tf_op jit(solution)/shard_map/write_out/pallas_call | solution.py:582

commit v11 on v8

--- a/solution.py
+++ b/solution.py
@@ -62,9 +62,10 @@
 
 def mix(spread_ref, x, first):
     sums = [first, None]
-    for k in range(C):
+    for step in range(C):
+        k = step % 4 * 8 + step // 4
         term = spread_ref[k] * jnp.broadcast_to(x[k : k + 1, :], (C, LANES))
-        sums[k % 2] = term if sums[k % 2] is None else sums[k % 2] + term
+        sums[step % 2] = term if sums[step % 2] is None else sums[step % 2] + term
     return sums[0] + sums[1]
 
 
@@ -224,10 +225,8 @@
 
     @pl.when(starts)
     def _():
-        def send(c, _):
+        for c in range(chunks):
             first_copy(c).start()
-            return 0
-        lax.fori_loop(0, chunks, send, 0)
 
     def propagator(matrix_ref, back_ref, row):
         spread(w_ref[0], matrix_ref)

time: 58.8 us -> 58.3 us (level)
  no operation moved by 1% of the time
where the time goes in v11:
time: 58.3 us; the launch traced here: 58.1 us
  Pallas kernels  57.4 us (98%)
  between operations  0.64 us (1%)
    pallas_call x1, Pallas kernels, body(): pl.pallas_call(kernel, out_shape=(image_shape, image_shape, jax.ShapeDtyp...  56.4 us

profile of v11, /device:TPU:103, one launch (start us, length us, event | category | flops | bytes accessed | tf_op | source)
XLA Modules:
  0.0 58.1 jit_solution(6868700269449671119)
XLA Ops:
  0.6 56.4 %mgrit_cycle.1 = (f32[32,4096]{1,0:T(8,128)S(1)}, f32[32,4096]{1,0:T(8,128)S(1)}, f32[8,32,32]{2,1,0:T(8,128)S(1)}, f32[8,32]{1,0:T(8,128)S(1)}) custom-call(f32[32,4096]{1,0:T(8,128)} %bitcast.5, f32[32,4096]{1,0:T(8,128)} %bitcast.6, f32[8,32,32]{2,1,0:T(8,128)} %w_hbm.1, f32[8,32]{1,0:T(8,128)} %b_hbm.1, f32[1,32]{1,0:T(1,128)} %bitcast.7, s32[32]{0:T(128)} %n_hbm.1), custom_call_target="tpu_custom_call" | custom-call | tf_op jit(solution)/shard_map/mgrit_cycle/pallas_call | solution.py:544
  57.0 1.0 %write_out.1 = (f32[32,4096]{1,0:T(8,128)}, f32[32,4096]{1,0:T(8,128)}, f32[8,32,32]{2,1,0:T(8,128)}, f32[8,32]{1,0:T(8,128)}) custom-call(f32[32,4096]{1,0:T(8,128)S(1)} %get-tuple-element.12.refs_0_, f32[32,4096]{1,0:T(8,128)S(1)} %get-tuple-element.13.refs_1_, f32[8,32,32]{2,1,0:T(8,128)S(1)} %get-tuple-element.14.refs_2_, ...), custom_call_target="tpu_custom_call" | custom-call | tf_op jit(solution)/shard_map/write_out/pallas_call | solution.py:579
